TPU v7x, 256 devices: a whole 4x4x8 slice. The times are simulated.
256 devices in a mesh: dev: 8 (over z), ha: 4 (over y), wa: 8 (over x, core).
Axes of the slice: x: 4, y: 4, z: 8, core: 2. Of those that a mesh axis runs over, the one named last changes fastest.
Arguments:
- volume: float32 [32, 32, 64, 256], P('dev', 'ha', 'wa'), may hold values from -6 to 6
- kernel: float32 [256, 27, 256], replicated, may hold values from -0.078125 to 0.078125
- upstream: float32 [32, 32, 64, 256], P('dev', 'ha', 'wa'), may hold values from -6 to 6
Outputs:
- output: float32 [32, 32, 64, 256], P('dev', 'ha', 'wa')
- volume_grad: float32 [32, 32, 64, 256], P('dev', 'ha', 'wa')
- kernel_grad: float32 [256, 27, 256], P('wa')
All inputs are finite; a program needn't handle non-finite values.
Results may differ from a plain program's by a relative error of at most 0.0001.
Values sent between devices are 32-bit elements; how exact they have to be, the bound alone decides.
A program may use at most 128 MiB of HBM per device.

v0:
```python
import math

import jax
import jax.numpy as jnp
from jax import lax
from jax.sharding import PartitionSpec as P


def padded_2(shard, sides, width):
    for axis, dim in sides:
        count, length = (lax.axis_size(axis), shard.shape[dim])
        up = [(i, (i + 1) % count) for i in range(count)]
        down = [(j, i) for i, j in up]
        last = lax.slice_in_dim(shard, length - width, length, axis=dim)
        initial = lax.slice_in_dim(shard, 0, width, axis=dim)
        before = lax.ppermute(last, axis, up)
        after = lax.ppermute(initial, axis, down)
        shard = jnp.concatenate([before, shard, after], axis=dim)
    return shard


def tap_offsets():
    return [(da, db, dc) for da in (-1, 0, 1) for db in (-1, 0, 1) for dc in (-1, 0, 1)]


def per_device(volume, kernel, upstream):
    depth_cells, height_cells, width_cells, channels = volume.shape
    cells = depth_cells * height_cells * width_cells
    stacked = jnp.stack([volume, upstream])
    padded = padded_2(stacked, (("dev", 1), ("ha", 2), ("wa", 3)), 1)
    forward_windows = []
    backward_windows = []
    for da, db, dc in tap_offsets():
        forward_windows.append(
            padded[
                0,
                1 + da : 1 + da + depth_cells,
                1 + db : 1 + db + height_cells,
                1 + dc : 1 + dc + width_cells,
            ].reshape(cells, channels)
        )
        backward_windows.append(
            padded[
                1,
                1 - da : 1 - da + depth_cells,
                1 - db : 1 - db + height_cells,
                1 - dc : 1 - dc + width_cells,
            ].reshape(cells, channels)
        )
    forward_patches = jnp.stack(forward_windows, axis=1)
    backward_patches = jnp.stack(backward_windows, axis=1)
    output = jnp.einsum(
        "ntc,cto->no",
        forward_patches,
        kernel,
        precision=lax.Precision.HIGHEST,
        preferred_element_type=jnp.float32,
    )
    volume_grad = jnp.einsum(
        "nto,cto->nc",
        backward_patches,
        kernel,
        precision=lax.Precision.HIGHEST,
        preferred_element_type=jnp.float32,
    )
    flat_up = upstream.reshape(cells, channels)
    total_cells = cells * lax.axis_size("dev") * lax.axis_size("ha") * lax.axis_size("wa")
    factor = 1.0 / math.sqrt(total_cells)
    owned = channels // lax.axis_size("wa")
    summed = lax.psum(
        jnp.einsum(
            "ntc,no->cto",
            forward_patches,
            flat_up,
            precision=lax.Precision.HIGHEST,
            preferred_element_type=jnp.float32,
        )
        * factor,
        ("dev", "ha", "wa"),
    )
    kernel_grad = lax.dynamic_slice_in_dim(summed, lax.axis_index("wa") * owned, owned, 0)
    return (output.reshape(volume.shape), volume_grad.reshape(volume.shape), kernel_grad)


def solution(mesh):
    placed = (P("dev", "ha", "wa", None), P(), P("dev", "ha", "wa", None))
    return jax.shard_map(
        per_device,
        mesh=mesh,
        in_specs=placed,
        out_specs=(P("dev", "ha", "wa", None), P("dev", "ha", "wa", None), P("wa", None, None)),
        check_vma=False,
    )
```

profile of v0, /device:TPU:2, one launch (start us, length us, event | category | flops | bytes accessed | tf_op | source)
XLA Modules:
  0.0 338.1 jit_solution(18164718943896220300)
XLA Ops:
  7.2 0.0 copy-start.2
  7.2 0.0 copy-start.1
  7.2 0.0 all-reduce.2.cloned.1.call-start
  7.2 1.0 pad_maximum_fusion.9
  8.2 2.0 collective-permute-start
  10.2 4.0 %collective-permute-start.1 = (f32[2,1,8,8,256]{4,3,2,1,0:T(8,128)S(1)}, f32[2,1,8,8,256]{4,3,2,1,0:T(8,128)S(1)}, u32[]{:S(2)}, u32[]{:S(2)}) collective-permute-start(f32[2,1,8,8,256]{4,3,2,1,0:T(8,128)S(1)} %get-tuple-element.66), channel_id=1, source_target_pairs={{32,0},{64,32},{96,64},{128,96},{160,128},{192,160},{224,192},{0,2... | collective-permute-start | bytes 393224 | tf_op jit(solution)/shard_map/ppermute | solution.py:17
  14.3 3.4 %collective-permute-done = f32[2,1,8,8,256]{4,3,2,1,0:T(8,128)S(1)} collective-permute-done((f32[2,1,8,8,256]{4,3,2,1,0:T(8,128)S(1)}, f32[2,1,8,8,256]{4,3,2,1,0:T(8,128)S(1)}, u32[]{:S(2)}, u32[]{:S(2)}) %collective-permute-start) | collective-permute-done | bytes 131104 | tf_op jit(solution)/shard_map/ppermute | solution.py:16
  17.7 0.0 collective-permute-done.1
  17.7 0.8 pad_maximum_fusion.19
  18.5 1.7 collective-permute-start.2
  20.2 1.7 collective-permute-start.3
  21.9 2.0 pad_maximum_fusion.2
  23.9 0.5 collective-permute-done.2
  24.4 0.4 collective-permute-done.3
  24.8 1.4 pad_maximum_fusion.10
  26.2 0.0 collective-permute-start.4
  26.2 1.7 collective-permute-start.5
  27.9 1.4 pad_maximum_fusion.1
  29.3 1.3 fusion.2
  30.6 0.0 collective-permute-done.4
  30.6 0.0 collective-permute-done.5
  30.6 0.6 pad_maximum_fusion
  31.3 1.5 fusion.1
  32.7 0.7 constant_dynamic-update-slice_fusion.53
  33.5 1.5 fusion
  35.7 2.8 copy-done
  38.5 13.7 %multiply_bitcast_fusion = f32[256,27,256]{2,0,1:T(8,128)} fusion(f32[256,27,256]{2,0,1:T(8,128)S(1)} %constant_dynamic-update-slice_fusion, f32[256,256,1]{1,0,2:T(8,128)S(1)} %bitcast.83), kind=kOutput, calls=%fused_computation | convolution fusion | flops 5437587456 | bytes 14417920 | tf_op jit(solution)/shard_map/ntc,no->cto/dot_general | solution.py:71
  52.2 0.0 all-reduce.2.cloned.1.call-update
  52.3 0.0 copy-start.13
  52.3 0.0 copy-start.8
  52.3 0.0 copy-start.12
  52.3 0.0 copy-start.9
  52.3 1.8 constant_dynamic-update-slice_fusion.52
  54.1 1.7 constant_dynamic-update-slice_fusion.51
  55.8 1.7 constant_dynamic-update-slice_fusion.50
  57.5 1.7 constant_dynamic-update-slice_fusion.49
  59.1 1.7 constant_dynamic-update-slice_fusion.48
  60.8 1.7 constant_dynamic-update-slice_fusion.47
  62.5 1.8 constant_dynamic-update-slice_fusion.46
  64.3 1.7 constant_dynamic-update-slice_fusion.45
  66.0 1.7 constant_dynamic-update-slice_fusion.44
  67.7 1.7 constant_dynamic-update-slice_fusion.43
  69.3 1.7 constant_dynamic-update-slice_fusion.42
  71.0 1.7 constant_dynamic-update-slice_fusion.41
  72.7 0.7 constant_dynamic-update-slice_fusion.40
  73.5 1.7 constant_dynamic-update-slice_fusion.39
  75.1 0.7 constant_dynamic-update-slice_fusion.38
  75.9 0.0 copy-done.6
  75.9 0.7 constant_dynamic-update-slice_fusion.37
  76.6 0.7 constant_dynamic-update-slice_fusion.36
  77.3 0.7 constant_dynamic-update-slice_fusion.35
  78.1 0.7 constant_dynamic-update-slice_fusion.34
  78.8 0.7 constant_dynamic-update-slice_fusion.33
  79.5 0.0 copy-done.8
  79.5 0.7 constant_dynamic-update-slice_fusion.32
  80.2 0.7 constant_dynamic-update-slice_fusion.31
  81.0 0.7 constant_dynamic-update-slice_fusion.30
  81.7 0.7 constant_dynamic-update-slice_fusion.29
  82.4 0.7 constant_dynamic-update-slice_fusion.28
  83.1 0.7 constant_dynamic-update-slice_fusion.27
  83.9 14.6 %fusion.4 = f32[256,256,1]{1,0,2:T(8,128)} fusion(f32[256,27,256]{2,0,1:T(8,128)S(1)} %bitcast.74, f32[256,27,256]{2,0,1:T(8,128)} %param.4), kind=kOutput, calls=%fused_computation.82 | convolution fusion | flops 5435817984 | bytes 14417920 | tf_op jit(solution)/shard_map/ntc,cto->no/dot_general | solution.py:52
  98.5 6.5 %fusion.5 = f32[256,256,1]{1,0,2:T(8,128)} fusion(f32[256,27,256]{2,0,1:T(8,128)S(1)} %copy-done.3, f32[256,27,256]{2,0,1:T(8,128)S(1)} %bitcast.76), kind=kOutput, calls=%fused_computation.83 | convolution fusion | flops 5435817984 | bytes 14417920 | tf_op jit(solution)/shard_map/nto,cto->nc/dot_general | solution.py:59
  105.1 224.1 %all-reduce.2.cloned.1.call-done = f32[256,27,256]{2,0,1:T(8,128)} async-done(((f32[256,27,256]{2,0,1:T(8,128)}), f32[256,27,256]{2,0,1:T(8,128)}) %all-reduce.2.cloned.1.call-update) | async-done | bytes 7077904 | tf_op jit(solution)/shard_map/psum | solution.py:70
  329.1 2.2 constant_dynamic-slice_fusion
  (58 shorter events, 0.6 us)
Async XLA Ops:
  7.2 23.5 %copy-start.2 = (f32[4,8,8,256]{3,2,1,0:T(8,128)S(1)}, f32[4,8,8,256]{3,2,1,0:T(8,128)}, u32[]{:S(2)}) copy-start(f32[4,8,8,256]{3,2,1,0:T(8,128)} %param.3) | copy-start | bytes 786436
  7.2 23.4 %copy-start.1 = (f32[4,8,8,256]{3,2,1,0:T(8,128)S(1)}, f32[4,8,8,256]{3,2,1,0:T(8,128)}, u32[]{:S(2)}) copy-start(f32[4,8,8,256]{3,2,1,0:T(8,128)} %param.5) | copy-start | bytes 786436
  7.2 321.9 %all-reduce.2.cloned.1.call-start = ((), (), s32[]{:S(2)}) async-start(), calls=%async_computation | async-start | bytes 14155776 | tf_op jit(solution)/shard_map/psum | solution.py:70
  8.2 9.4 %collective-permute-start = (f32[2,1,8,8,256]{4,3,2,1,0:T(8,128)S(1)}, f32[2,1,8,8,256]{4,3,2,1,0:T(8,128)S(1)}, u32[]{:S(2)}, u32[]{:S(2)}) collective-permute-start(f32[2,1,8,8,256]{4,3,2,1,0:T(8,128)S(1)} %get-tuple-element.65), channel_id=1, source_target_pairs={{0,32},{32,64},{64,96},{96,128},{128,160},{160,192},{192,224},{224... | collective-permute-start | bytes 393224 | tf_op jit(solution)/shard_map/ppermute | solution.py:16
  10.2 7.4 %collective-permute-start.1 = (f32[2,1,8,8,256]{4,3,2,1,0:T(8,128)S(1)}, f32[2,1,8,8,256]{4,3,2,1,0:T(8,128)S(1)}, u32[]{:S(2)}, u32[]{:S(2)}) collective-permute-start(f32[2,1,8,8,256]{4,3,2,1,0:T(8,128)S(1)} %get-tuple-element.66), channel_id=1, source_target_pairs={{32,0},{64,32},{96,64},{128,96},{160,128},{192,160},{224,192},{0,2... | collective-permute-start | bytes 393224 | tf_op jit(solution)/shard_map/ppermute | solution.py:17
  18.5 5.9 %collective-permute-start.2 = (f32[2,6,1,8,256]{4,3,2,1,0:T(8,128)S(1)}, f32[2,6,1,8,256]{4,3,2,1,0:T(8,128)S(1)}, u32[]{:S(2)}, u32[]{:S(2)}) collective-permute-start(f32[2,6,1,8,256]{4,3,2,1,0:T(8,128)S(1)} %get-tuple-element.57), channel_id=1, source_target_pairs={{0,8},{8,16},{16,24},{24,0},{1,9},{9,17},{17,25},{25,1},{2,10},{10... | collective-permute-start | bytes 294920 | tf_op jit(solution)/shard_map/ppermute | solution.py:16
  20.2 4.6 %collective-permute-start.3 = (f32[2,6,1,8,256]{4,3,2,1,0:T(8,128)S(1)}, f32[2,6,1,8,256]{4,3,2,1,0:T(8,128)S(1)}, u32[]{:S(2)}, u32[]{:S(2)}) collective-permute-start(f32[2,6,1,8,256]{4,3,2,1,0:T(8,128)S(1)} %get-tuple-element.58), channel_id=1, source_target_pairs={{8,0},{16,8},{24,16},{0,24},{9,1},{17,9},{25,17},{1,25},{10,2},{18... | collective-permute-start | bytes 294920 | tf_op jit(solution)/shard_map/ppermute | solution.py:17
  26.2 4.4 %collective-permute-start.4 = (f32[2,6,10,1,256]{4,3,2,1,0:T(1,128)S(1)}, f32[2,6,10,1,256]{4,3,2,1,0:T(1,128)S(1)}, u32[]{:S(2)}, u32[]{:S(2)}) collective-permute-start(f32[2,6,10,1,256]{4,3,2,1,0:T(1,128)S(1)} %get-tuple-element.42), channel_id=1, source_target_pairs={{0,1},{1,2},{2,3},{3,4},{4,5},{5,6},{6,7},{7,0},{8,9},{9,10},{10,1... | collective-permute-start | bytes 368648 | tf_op jit(solution)/shard_map/ppermute | solution.py:16
  26.2 4.4 %collective-permute-start.5 = (f32[2,6,10,1,256]{4,3,2,1,0:T(1,128)S(1)}, f32[2,6,10,1,256]{4,3,2,1,0:T(1,128)S(1)}, u32[]{:S(2)}, u32[]{:S(2)}) collective-permute-start(f32[2,6,10,1,256]{4,3,2,1,0:T(1,128)S(1)} %get-tuple-element.41), channel_id=1, source_target_pairs={{1,0},{2,1},{3,2},{4,3},{5,4},{6,5},{7,6},{0,7},{9,8},{10,9},{11,1... | collective-permute-start | bytes 368648 | tf_op jit(solution)/shard_map/ppermute | solution.py:17
  35.7 2.8 copy-start
  52.2 31.7 %slice-start = ((s8[7077888]{0:T(1024)(128)(4,1)}), s8[2883584]{0:T(1024)(128)(4,1)S(1)}, s32[]{:S(2)}) async-start(s8[7077888]{0:T(1024)(128)(4,1)} %bitcast.73), calls=%async_computation.1 | async-start | bytes 5767168
  52.2 22.9 %copy-start.11 = (f32[1,4,8,8,256]{4,3,2,1,0:T(8,128)S(1)}, f32[1,4,8,8,256]{4,3,2,1,0:T(8,128)}, u32[]{:S(2)}) copy-start(f32[1,4,8,8,256]{4,3,2,1,0:T(8,128)} %get-tuple-element.24) | copy-start | bytes 786436
  52.2 23.7 %copy-start.6 = (f32[1,4,8,8,256]{4,3,2,1,0:T(8,128)S(1)}, f32[1,4,8,8,256]{4,3,2,1,0:T(8,128)}, u32[]{:S(2)}) copy-start(f32[1,4,8,8,256]{4,3,2,1,0:T(8,128)} %get-tuple-element.44) | copy-start | bytes 786436
  52.2 24.4 %copy-start.14 = (f32[1,4,8,8,256]{4,3,2,1,0:T(8,128)S(1)}, f32[1,4,8,8,256]{4,3,2,1,0:T(8,128)}, u32[]{:S(2)}) copy-start(f32[1,4,8,8,256]{4,3,2,1,0:T(8,128)} %get-tuple-element.6) | copy-start | bytes 786436
  52.2 25.1 %copy-start.10 = (f32[1,4,8,8,256]{4,3,2,1,0:T(8,128)S(1)}, f32[1,4,8,8,256]{4,3,2,1,0:T(8,128)}, u32[]{:S(2)}) copy-start(f32[1,4,8,8,256]{4,3,2,1,0:T(8,128)} %get-tuple-element.23) | copy-start | bytes 786436
  52.2 25.8 %copy-start.5 = (f32[1,4,8,8,256]{4,3,2,1,0:T(8,128)S(1)}, f32[1,4,8,8,256]{4,3,2,1,0:T(8,128)}, u32[]{:S(2)}) copy-start(f32[1,4,8,8,256]{4,3,2,1,0:T(8,128)} %get-tuple-element.72) | copy-start | bytes 786436
  52.3 26.5 %copy-start.13 = (f32[1,4,8,8,256]{4,3,2,1,0:T(8,128)S(1)}, f32[1,4,8,8,256]{4,3,2,1,0:T(8,128)}, u32[]{:S(2)}) copy-start(f32[1,4,8,8,256]{4,3,2,1,0:T(8,128)} %get-tuple-element.5) | copy-start | bytes 786436
  52.3 27.2 %copy-start.8 = (f32[1,4,8,8,256]{4,3,2,1,0:T(8,128)S(1)}, f32[1,4,8,8,256]{4,3,2,1,0:T(8,128)}, u32[]{:S(2)}) copy-start(f32[1,4,8,8,256]{4,3,2,1,0:T(8,128)} %get-tuple-element.22) | copy-start | bytes 786436
  52.3 28.7 %copy-start.12 = (f32[1,4,8,8,256]{4,3,2,1,0:T(8,128)S(1)}, f32[1,4,8,8,256]{4,3,2,1,0:T(8,128)}, u32[]{:S(2)}) copy-start(f32[1,4,8,8,256]{4,3,2,1,0:T(8,128)} %get-tuple-element.4) | copy-start | bytes 786436
  52.3 29.4 %copy-start.7 = (f32[1,4,8,8,256]{4,3,2,1,0:T(8,128)S(1)}, f32[1,4,8,8,256]{4,3,2,1,0:T(8,128)}, u32[]{:S(2)}) copy-start(f32[1,4,8,8,256]{4,3,2,1,0:T(8,128)} %get-tuple-element.21) | copy-start | bytes 786436
  52.3 30.1 %copy-start.4 = (f32[1,4,8,8,256]{4,3,2,1,0:T(8,128)S(1)}, f32[1,4,8,8,256]{4,3,2,1,0:T(8,128)}, u32[]{:S(2)}) copy-start(f32[1,4,8,8,256]{4,3,2,1,0:T(8,128)} %get-tuple-element.43) | copy-start | bytes 786436
  52.3 30.8 %copy-start.9 = (f32[1,4,8,8,256]{4,3,2,1,0:T(8,128)S(1)}, f32[1,4,8,8,256]{4,3,2,1,0:T(8,128)}, u32[]{:S(2)}) copy-start(f32[1,4,8,8,256]{4,3,2,1,0:T(8,128)} %get-tuple-element.3) | copy-start | bytes 786436
  62.5 21.4 %slice-start.1 = ((s8[7077888]{0:T(1024)(128)(4,1)}), s8[4194304]{0:T(1024)(128)(4,1)S(1)}, s32[]{:S(2)}) async-start(s8[7077888]{0:T(1024)(128)(4,1)} %bitcast.73), calls=%async_computation.2 | async-start | bytes 8388608
  82.4 16.1 %slice-start.2 = ((s8[7077888]{0:T(1024)(128)(4,1)}), s8[4194304]{0:T(1024)(128)(4,1)S(1)}, s32[]{:S(2)}) async-start(s8[7077888]{0:T(1024)(128)(4,1)} %bitcast.75), calls=%async_computation.3 | async-start | bytes 8388608
  83.9 14.7 %slice-start.3 = ((s8[7077888]{0:T(1024)(128)(4,1)}), s8[2883584]{0:T(1024)(128)(4,1)S(1)}, s32[]{:S(2)}) async-start(s8[7077888]{0:T(1024)(128)(4,1)} %bitcast.75), calls=%async_computation.4 | async-start | bytes 5767168
  83.9 14.7 %copy-start.3 = (f32[256,27,256]{2,0,1:T(8,128)S(1)}, f32[256,27,256]{2,0,1:T(8,128)}, u32[]{:S(2)}) copy-start(f32[256,27,256]{2,0,1:T(8,128)} %constant_dynamic-update-slice_fusion.27) | copy-start | bytes 21233668
Sparse Core Ops, SparseCore 0:
  52.3 276.7 all-reduce.1
where the time goes:
time: 339 us; the launch traced here: 338 us
  waiting for transfers between devices  228 us (67%)
  local copies, waits for them, and re-layouts  42.1 us (12%)
  matrix products  34.9 us (10%)
  between operations  14.4 us (4%)
  starting transfers between devices  11.2 us (3%)
  other arithmetic  7.22 us (2%)
    psum x1, waiting for transfers between devices, per_device(): lax.psum(jnp.einsum('ntc,no->cto', forward_patches, flat_up, precision=la...  224 us
    unnamed x90, local copies, waits for them, and re-layouts  34.9 us
    dot_general x1, matrix products, per_device(): jnp.einsum('ntc,cto->no', forward_patches, kernel, precision=lax.Precisio...  14.6 us
    dot_general x1, matrix products, per_device(): jnp.einsum('ntc,no->cto', forward_patches, flat_up, precision=lax.Precisi...  13.7 us
    ppermute x3, starting transfers between devices, padded_2(): after = lax.ppermute(initial, axis, down)  7.47 us
  transfers between devices with their start and end apart: 7, of which 4 were waited for; matrix products, arithmetic and copies ran while one was open for 17% of the time, Pallas kernels for 0%

commit v1 on v0

v1 whole, which is shorter than its diff:
```python
import functools
import math

import jax
import jax.numpy as jnp
from jax import lax
from jax.experimental import pallas as pl
from jax.experimental.pallas import tpu as pltpu
from jax.sharding import PartitionSpec as P

MESH = pl.DeviceIdType.MESH
F32 = jnp.float32
BF16 = jnp.bfloat16

GROUPS = 7
FIRST = ("x", "y", "x", "y", "x", "y", "x")
BATCHES = ((0, 4), (4, 7))
N_SEM = 2 * 10 + GROUPS + GROUPS * 8 + len(BATCHES) * (7 + 7 + 4)


def split(x):
    hi = x.astype(BF16)
    return hi, (x - hi.astype(F32)).astype(BF16)


def dot3(lhs, rhs, dims):
    (lh, ll), (rh, rl) = lhs, rhs
    dot = functools.partial(
        lax.dot_general, dimension_numbers=(dims, ((), ())), preferred_element_type=F32
    )
    return dot(lh, rh) + (dot(ll, rh) + dot(lh, rl))


def kernel(
    factor,
    vol_ref, up_ref, k_hbm, out_ref, vg_ref, kg_ref,
    k_f, pad_v, pad_u, col_v, col_u, halo_v, halo_u,
    wv_hi, wv_lo, wu_hi, wu_lo, vt_hi, vt_lo, acc_o, acc_g,
    part, pair, summed, r1, s2, r2, mid, q1, t2, q2, low, rz, fin, agz, full,
    ksem, send_sem, recv_sem,
):
    z, y, w = lax.axis_index("dev"), lax.axis_index("ha"), lax.axis_index("wa")
    core = lax.rem(w, 2)
    x = lax.div(w, 2)

    def step(i, by, n):
        return lax.rem(i + (by + n), n)

    counter = [0]
    sent = []

    def copy(src, dst, device):
        i = counter[0]
        counter[0] += 1
        return pltpu.make_async_remote_copy(
            src_ref=src, dst_ref=dst, send_sem=send_sem.at[i], recv_sem=recv_sem.at[i],
            device_id=device, device_id_type=MESH,
        )

    def start(*copies):
        for c in copies:
            c.start()
            sent.append(c)
        return copies

    k_copies = [
        pltpu.make_async_copy(k_hbm.at[pl.ds(9 * i, 9)], k_f.at[pl.ds(9 * i, 9)], ksem.at[i])
        for i in range(3)
    ]
    for c in k_copies:
        c.start()

    peers = []
    for sd in (-1, 0, 1):
        for sh in (-1, 0, 1):
            if (sd, sh) != (0, 0):
                peers.append({"dev": step(z, sd, 8), "ha": step(y, sh, 4)})
    for k in range(2, 7):
        peers.append({"dev": step(z, k, 8)})
    for k in (-2, -1, 1, 2):
        peers.append({"wa": step(w, k, 8)})
    barrier = pltpu.get_barrier_semaphore()
    for peer in peers:
        pl.semaphore_signal(barrier, inc=1, device_id=peer, device_id_type=MESH)
    pad_u[1:5, 1:9] = up_ref[...]
    pad_v[1:5, 1:9] = vol_ref[...]
    pl.semaphore_wait(barrier, len(peers))

    def send_faces(src, pad):
        copies = []
        for sd in (-1, 0, 1):
            for sh in (-1, 0, 1):
                if (sd, sh) == (0, 0):
                    continue
                d_src, d_dst, d_n = ((0, 5, 1), (0, 1, 4), (3, 0, 1))[sd + 1]
                h_src, h_dst, h_n = ((0, 9, 1), (0, 1, 8), (7, 0, 1))[sh + 1]
                copies.append(copy(
                    src.at[pl.ds(d_src, d_n), pl.ds(h_src, h_n)],
                    pad.at[pl.ds(d_dst, d_n), pl.ds(h_dst, h_n)],
                    {"dev": step(z, sd, 8), "ha": step(y, sh, 4)},
                ))
        return start(*copies)

    def send_columns(pad, col, halo):
        col[0] = pad[:, :, 0:1, :]
        col[1] = pad[:, :, 7:8, :]
        return start(
            copy(col.at[0], halo.at[1], {"wa": step(w, -1, 8)}),
            copy(col.at[1], halo.at[0], {"wa": step(w, 1, 8)}),
        )

    def arrive(copies):
        for c in copies:
            c.wait_recv()

    def windows(pad, halo, hi_ref, lo_ref):
        def body(d, carry):
            rows = pl.ds(pl.multiple_of(d * 64, 64), 64)
            plane = pad[d]
            at = lax.broadcasted_iota(jnp.int32, plane.shape, 1)
            before = jnp.broadcast_to(halo[0, d], plane.shape)
            after = jnp.broadcast_to(halo[1, d], plane.shape)
            shifted = (
                jnp.where(at == 0, before, pltpu.roll(plane, 1, 1)),
                plane,
                jnp.where(at == 7, after, pltpu.roll(plane, 7, 1)),
            )
            for b in range(3):
                for c in range(3):
                    hi, lo = split(shifted[c][b : b + 8].reshape(64, plane.shape[-1]))
                    hi_ref[3 * b + c, rows, :] = hi
                    lo_ref[3 * b + c, rows, :] = lo
            return carry

        lax.fori_loop(0, 6, body, 0)

    def window(hi_ref, lo_ref, t):
        rows = pl.ds(pl.multiple_of(lax.div(t, 9) * 64, 64), 256)
        i = lax.rem(t, 9)
        return hi_ref[i, rows, :], lo_ref[i, rows, :]

    def kernel_grad(g):
        def body(i, carry):
            t = 4 * g + i
            upwin = window(wu_hi, wu_lo, 26 - t)
            res = dot3((vt_hi[...], vt_lo[...]), upwin, ((1,), (0,)))
            for block in range(8):
                for half in range(2):
                    part[g, block % 2, block // 2, 2 * i + half] = res[
                        32 * block : 32 * block + 32, 128 * half : 128 * half + 128
                    ]
            return carry

        taps = min(4, 27 - 4 * g)
        lax.fori_loop(0, taps, body, 0)
        for i in range(taps, 4):
            for j in (2 * i, 2 * i + 1):
                part[g, :, :, j] = jnp.zeros((2, 4, 32, 128), F32)

    def products(first, last):
        def body(t, carry):
            k = split(k_f[t])
            acc_o[...] += dot3(window(wv_hi, wv_lo, t), k, ((1,), (0,)))
            acc_g[...] += dot3(window(wu_hi, wu_lo, 26 - t), k, ((1,), (1,)))
            return carry

        lax.fori_loop(first, last, body, 0)

    def ring_devices(axis):
        if axis == "x":
            return x, {"wa": step(w, 2, 8)}, {"wa": step(w, -2, 8)}
        return y, {"ha": step(y, 1, 4)}, {"ha": step(y, -1, 4)}

    def ring_1(axis, chunk, recv):
        i, up, down = ring_devices(axis)
        far = chunk(step(i, 2, 4))
        return start(
            copy(halves(far, 0), recv.at[0], up),
            copy(halves(far, 1), recv.at[1], down),
        )

    def halves(ref, h):
        if len(ref.shape) == 4:
            return ref.at[:, pl.ds(4 * h, 4)]
        return ref.at[pl.ds(4 * h, 4)]

    def ring_2(axis, copies, chunk, recv, stage, recv_2):
        i, up, down = ring_devices(axis)
        arrive(copies)
        for h, by in ((0, 1), (1, -1)):
            near = chunk(step(i, by, 4))
            halves(stage.at[h], h)[...] = halves(near, h)[...] + recv[h]
            halves(stage.at[h], 1 - h)[...] = halves(near, 1 - h)[...]
        return start(copy(stage.at[0], recv_2.at[0], up), copy(stage.at[1], recv_2.at[1], down))

    def ring_3(axis, copies, chunk, recv_2):
        i, _, _ = ring_devices(axis)
        arrive(copies)
        return chunk(i)[...] + recv_2[0] + recv_2[1]

    def rows_of(ref, k):
        rows = pl.ds(pl.multiple_of(k * 8, 8), 8)
        if len(ref.shape) == 4:
            return ref.at[:, :, rows]
        return ref.at[:, rows]

    class Group:
        def __init__(self, g):
            self.g = g
            self.first = FIRST[g]
            self.second = "y" if self.first == "x" else "x"
            n = FIRST[:g].count(self.first)
            i = 0 if self.first == "x" else 1
            self.r1, self.s2, self.r2 = r1[i].at[n], s2[i].at[n], r2[i].at[n]
            self.mid = mid[i].at[n]
            self.sum = summed.at[g]
            self.q1, self.t2, self.q2 = q1.at[g], t2.at[g], q2.at[g]
            if self.first == "x":
                self.chunk_1 = lambda k: self.sum.at[k]
                self.chunk_2 = lambda k: rows_of(self.mid, k)
            else:
                self.chunk_1 = lambda k: rows_of(self.sum, k)
                self.chunk_2 = lambda k: self.mid.at[k]

        def pair(self):
            self.c = start(copy(part.at[self.g, 1 - core], pair.at[self.g], {"wa": w + 1 - 2 * core}))

        def e1(self):
            arrive(self.c)
            self.sum[...] = part[self.g, core] + pair[self.g]
            self.c = ring_1(self.first, self.chunk_1, self.r1)

        def e2(self):
            self.c = ring_2(self.first, self.c, self.chunk_1, self.r1, self.s2, self.r2)

        def e3(self):
            self.mid[...] = ring_3(self.first, self.c, self.chunk_1, self.r2)
            self.c = ring_1(self.second, self.chunk_2, self.q1)

        def e4(self):
            self.c = ring_2(self.second, self.c, self.chunk_2, self.q1, self.t2, self.q2)

        def e5(self):
            low[self.g] = ring_3(self.second, self.c, self.chunk_2, self.q2)

    class Batch:
        def __init__(self, i):
            self.lo, self.hi = BATCHES[i]
            self.gs = pl.ds(self.lo, self.hi - self.lo)

        def e6(self):
            self.c = start(*(
                copy(low.at[self.gs, step(z, k, 8)], rz.at[k - 1, self.gs], {"dev": step(z, k, 8)})
                for k in range(1, 8)
            ))

        def e7(self):
            arrive(self.c)
            total = low[self.gs, z]
            for k in range(7):
                total = total + rz[k, self.gs]
            total = total * factor
            fin[self.gs] = total
            agz[self.gs, z] = total
            sends, self.c = [], []
            for k in range(1, 8):
                i = counter[0]
                sends.append(copy(fin.at[self.gs], agz.at[self.gs, z], {"dev": step(z, k, 8)}))
                self.c.append(pltpu.make_async_remote_copy(
                    src_ref=fin.at[self.gs], dst_ref=agz.at[self.gs, step(z, -k, 8)],
                    send_sem=send_sem.at[i], recv_sem=recv_sem.at[i],
                    device_id={"dev": step(z, k, 8)}, device_id_type=MESH,
                ))
            start(*sends)

        def landed(self, sends, slots):
            return [
                pltpu.make_async_remote_copy(
                    src_ref=slot, dst_ref=slot, send_sem=send_sem.at[i], recv_sem=recv_sem.at[i],
                    device_id={"ha": step(y, 1, 4)}, device_id_type=MESH,
                )
                for i, slot in zip(sends, slots)
            ]

        def e8(self):
            arrive(self.c)
            full[self.gs, :, y] = agz[self.gs]
            i = counter[0]
            mine = full.at[self.gs, :, y]
            start(
                copy(agz.at[self.gs], mine, {"ha": step(y, 1, 4)}),
                copy(agz.at[self.gs], mine, {"ha": step(y, -1, 4)}),
            )
            self.c = self.landed(
                (i, i + 1), (full.at[self.gs, :, step(y, -1, 4)], full.at[self.gs, :, step(y, 1, 4)])
            )

        def e9(self):
            arrive(self.c)
            i = counter[0]
            below = full.at[self.gs, pl.ds(0, 4), step(y, -1, 4)]
            above = full.at[self.gs, pl.ds(4, 4), step(y, 1, 4)]
            start(
                copy(below, below, {"ha": step(y, 1, 4)}),
                copy(above, above, {"ha": step(y, -1, 4)}),
            )
            far = step(y, 2, 4)
            self.c = self.landed(
                (i, i + 1), (full.at[self.gs, pl.ds(0, 4), far], full.at[self.gs, pl.ds(4, 4), far])
            )

        def e10(self):
            arrive(self.c)
            for g in range(self.lo, self.hi):
                for t in range(4 * g, min(4 * g + 4, 27)):
                    for half in range(2):
                        kg_ref[t, :, 128 * half : 128 * half + 128] = full[
                            g, 2 * (t - 4 * g) + half
                        ].reshape(32, 128)

    faces_u = send_faces(up_ref, pad_u)
    faces_v = send_faces(vol_ref, pad_v)
    hi, lo = split(vol_ref[...].reshape(256, 256).T)
    vt_hi[...] = hi
    vt_lo[...] = lo
    acc_o[...] = jnp.zeros_like(acc_o)
    acc_g[...] = jnp.zeros_like(acc_g)
    arrive(faces_u)
    cols_u = send_columns(pad_u, col_u, halo_u)
    arrive(faces_v)
    cols_v = send_columns(pad_v, col_v, halo_v)
    arrive(cols_u)
    windows(pad_u, halo_u, wu_hi, wu_lo)

    groups = [Group(g) for g in range(GROUPS)]
    batches = [Batch(i) for i in range(len(BATCHES))]
    for g in range(GROUPS):
        kernel_grad(g)
        groups[g].pair()
        if g >= 1:
            groups[g - 1].e1()
        if g >= 3:
            groups[g - 3].e2()
    groups[6].e1()
    arrive(cols_v)
    windows(pad_v, halo_v, wv_hi, wv_lo)
    for c in k_copies:
        c.wait()
    groups[4].e2()
    groups[0].e3()
    groups[1].e3()
    products(0, 5)
    groups[5].e2()
    groups[6].e2()
    groups[0].e4()
    groups[1].e4()
    products(5, 11)
    groups[2].e3()
    groups[3].e3()
    groups[0].e5()
    groups[1].e5()
    products(11, 16)
    groups[2].e4()
    groups[3].e4()
    products(16, 21)
    groups[4].e3()
    groups[5].e3()
    groups[2].e5()
    groups[3].e5()
    batches[0].e6()
    products(21, 27)
    out_ref[...] = acc_o[...].reshape(out_ref.shape)
    vg_ref[...] = acc_g[...].reshape(vg_ref.shape)
    groups[4].e4()
    groups[5].e4()
    groups[6].e3()
    batches[0].e7()
    groups[4].e5()
    groups[5].e5()
    groups[6].e4()
    batches[0].e8()
    groups[6].e5()
    batches[1].e6()
    batches[0].e9()
    batches[1].e7()
    batches[0].e10()
    batches[1].e8()
    batches[1].e9()
    batches[1].e10()
    assert counter[0] == N_SEM, counter[0]
    for c in sent:
        c.wait_send()


def per_device(factor, volume, kernel_taps, upstream):
    nx, ny = FIRST.count("x"), FIRST.count("y")
    vmem = pltpu.VMEM

    def both(tail, n_last=None):
        return tail

    scratch = [
        vmem((27, 256, 256), F32),
        vmem((6, 10, 8, 256), F32), vmem((6, 10, 8, 256), F32),
        vmem((2, 6, 10, 1, 256), F32), vmem((2, 6, 10, 1, 256), F32),
        vmem((2, 6, 10, 1, 256), F32), vmem((2, 6, 10, 1, 256), F32),
        vmem((9, 384, 256), BF16), vmem((9, 384, 256), BF16),
        vmem((9, 384, 256), BF16), vmem((9, 384, 256), BF16),
        vmem((256, 256), BF16), vmem((256, 256), BF16),
        vmem((256, 256), F32), vmem((256, 256), F32),
        vmem((GROUPS, 2, 4, 8, 32, 128), F32),
        vmem((GROUPS, 4, 8, 32, 128), F32),
        vmem((GROUPS, 4, 8, 32, 128), F32),
        [vmem((nx, 2, 4, 32, 128), F32), vmem((ny, 2, 4, 4, 8, 128), F32)],
        [vmem((nx, 2, 8, 32, 128), F32), vmem((ny, 2, 4, 8, 8, 128), F32)],
        [vmem((nx, 2, 8, 32, 128), F32), vmem((ny, 2, 4, 8, 8, 128), F32)],
        [vmem((nx, 8, 32, 128), F32), vmem((ny, 4, 8, 8, 128), F32)],
        vmem((GROUPS, 2, 4, 8, 128), F32),
        vmem((GROUPS, 2, 8, 8, 128), F32),
        vmem((GROUPS, 2, 8, 8, 128), F32),
        vmem((GROUPS, 8, 8, 128), F32),
        vmem((7, GROUPS, 8, 128), F32),
        vmem((GROUPS, 8, 128), F32),
        vmem((GROUPS, 8, 8, 128), F32),
        vmem((GROUPS, 8, 4, 8, 128), F32),
        pltpu.SemaphoreType.DMA((3,)),
        pltpu.SemaphoreType.DMA((N_SEM,)),
        pltpu.SemaphoreType.DMA((N_SEM,)),
    ]
    in_vmem = pl.BlockSpec(memory_space=pltpu.VMEM)
    output, volume_grad, kg = pl.pallas_call(
        functools.partial(kernel, factor),
        out_shape=(
            jax.ShapeDtypeStruct(volume.shape, F32),
            jax.ShapeDtypeStruct(volume.shape, F32),
            jax.ShapeDtypeStruct((27, 32, 256), F32),
        ),
        in_specs=[in_vmem, in_vmem, pl.BlockSpec(memory_space=pl.ANY)],
        out_specs=(in_vmem, in_vmem, in_vmem),
        scratch_shapes=scratch,
        compiler_params=pltpu.CompilerParams(
            collective_id=0, has_side_effects=True, vmem_limit_bytes=56 * 2**20
        ),
    )(volume, upstream, jnp.transpose(kernel_taps, (1, 0, 2)))
    return output, volume_grad, jnp.transpose(kg, (1, 0, 2))


def solution(mesh):
    cells = 256 * mesh.shape["dev"] * mesh.shape["ha"] * mesh.shape["wa"]
    place = P("dev", "ha", "wa", None)
    return jax.shard_map(
        functools.partial(per_device, 1.0 / math.sqrt(cells)),
        mesh=mesh,
        in_specs=(place, P(), place),
        out_specs=(place, place, P("wa", None, None)),
        check_vma=False,
    )
```

time: 339 us -> 88.9 us (0.26)
  waiting for transfers between devices: 228 us -> 0 us
  Pallas kernels: 0 us -> 82.5 us
  local copies, waits for them, and re-layouts: 42.1 us -> 5.52 us
  matrix products: 34.9 us -> 0 us
  between operations: 14.4 us -> 0.64 us
  starting transfers between devices: 11.2 us -> 0 us
  other arithmetic: 7.22 us -> 0 us
    psum x1 -> x0, waiting for transfers between devices: 224 us -> none  [per_device(): lax.psum(jnp.einsum('ntc,no->cto', forward_patches, flat_up, precision=la...]
    pallas_call x0 -> x1, Pallas kernels: none -> 82.5 us  [per_device(): pl.pallas_call(functools.partial(kernel, factor), out_shape=(jax.ShapeDty...]
    dot_general x3 -> x0, matrix products: 34.9 us -> none  [the longest x1 14.6 us: per_device(): jnp.einsum('ntc,cto->no', forward_patches, kernel, precision=lax.Precisio...]
    unnamed x90 -> x3, local copies, waits for them, and re-layouts: 34.9 us -> 5.52 us
    ppermute x6 -> x0, starting transfers between devices: 11.1 us -> none  [the longest x3 7.47 us: padded_2(): after = lax.ppermute(initial, axis, down)]
    concatenate x4 -> x0, other arithmetic: 5.39 us -> none  [padded_2(): shard = jnp.concatenate([before, shard, after], axis=dim)]
    ppermute x6 -> x0, waiting for transfers between devices: 4.33 us -> none  [the longest x3 3.95 us: padded_2(): before = lax.ppermute(last, axis, up)]
    slice x3 -> x0, local copies, waits for them, and re-layouts: 4.24 us -> none  [per_device(): padded[1, 1 - da:1 - da + depth_cells, 1 - db:1 - db + height_cells, 1 -...]
  transfers between devices with their start and end apart: 7 -> 0, of which waited for: 4 -> 0; matrix products, arithmetic and copies ran while one was open for 17% -> 0% of each run, Pallas kernels for 0% -> 0%
where the time goes in v1:
time: 88.9 us; the launch traced here: 88.7 us
  Pallas kernels  82.5 us (93%)
  local copies, waits for them, and re-layouts  5.52 us (6%)
    pallas_call x1, Pallas kernels, per_device(): pl.pallas_call(functools.partial(kernel, factor), out_shape=(jax.ShapeDty...  82.5 us
    unnamed x3, local copies, waits for them, and re-layouts  5.52 us

profile of v1, /device:TPU:2, one launch (start us, length us, event | category | flops | bytes accessed | tf_op | source)
XLA Modules:
  0.0 88.7 jit_solution(1283776153929295012)
XLA Ops:
  0.6 82.5 %shard_map.58 = (f32[4,8,8,256]{3,2,1,0:T(8,128)}, f32[4,8,8,256]{3,2,1,0:T(8,128)}, f32[27,32,256]{2,1,0:T(8,128)}) custom-call(f32[4,8,8,256]{3,2,1,0:T(8,128)} %vol_ref.1, f32[4,8,8,256]{3,2,1,0:T(8,128)} %up_ref.1, f32[27,256,256]{2,1,0:T(8,128)} %bitcast.2), custom_call_target="tpu_custom_call" | custom-call | tf_op jit(solution)/shard_map/pallas_call | solution.py:431
  83.2 1.7 %copy.9 = f32[4,8,8,256]{3,2,1,0:T(8,128)} copy(f32[4,8,8,256]{3,2,1,0:T(8,128)} %get-tuple-element.12) | data formatting | bytes 524288
  84.8 1.7 %copy.10 = f32[4,8,8,256]{3,2,1,0:T(8,128)} copy(f32[4,8,8,256]{3,2,1,0:T(8,128)} %get-tuple-element.13) | data formatting | bytes 524288
  86.5 2.2 %copy.11 = f32[32,27,256]{2,0,1:T(8,128)} copy(f32[32,27,256]{2,0,1:T(8,128)} %bitcast.3) | data formatting | bytes 1769472

commit v2 on v1

v2 whole, which is shorter than its diff:
```python
import functools
import math

import jax
import jax.numpy as jnp
from jax import lax
from jax.experimental import pallas as pl
from jax.experimental.pallas import tpu as pltpu
from jax.sharding import PartitionSpec as P

MESH = pl.DeviceIdType.MESH
F32 = jnp.float32
BF16 = jnp.bfloat16

GROUPS = 7
FIRST = ("z", "x", "y", "x", "y", "x", "y")
BATCHES = ((0, 4), (4, 7))
N_SEM = 2 * 10 + GROUPS + 6 * (2 + 2 + 3) + (7 + 3 + 3) + len(BATCHES) * (7 + 7 + 3)


def tap(u):
    if isinstance(u, int):
        return 3 * u + 1 if u < 9 else 3 * ((u - 9) // 2) + 2 * ((u - 9) % 2)
    v = jnp.maximum(u - 9, 0)
    return jnp.where(u < 9, 3 * u + 1, 3 * lax.div(v, 2) + 2 * lax.rem(v, 2))


def split(x):
    hi = x.astype(BF16)
    return hi, (x - hi.astype(F32)).astype(BF16)


def dot3(lhs, rhs, dims):
    (lh, ll), (rh, rl) = lhs, rhs
    dot = functools.partial(
        lax.dot_general, dimension_numbers=(dims, ((), ())), preferred_element_type=F32
    )
    return dot(lh, rh) + (dot(ll, rh) + dot(lh, rl))


def kernel(
    factor,
    vol_ref, up_ref, k_hbm, out_ref, vg_ref, kg_ref,
    k_f, pad_v, pad_u, col_v, col_u, halo_v, halo_u,
    wv_hi, wv_lo, wu_hi, wu_lo, vt_hi, vt_lo, acc_o, acc_g,
    part, pair, summed, r1, s2, r2, mid, q1, low, rz, fin, agz,
    z1, zmid, z2, zlow, z3,
    ksem, local_sem, send_sem, recv_sem,
):
    z, y, w = lax.axis_index("dev"), lax.axis_index("ha"), lax.axis_index("wa")
    core = lax.rem(w, 2)
    x = lax.div(w, 2)

    def step(i, by, n):
        return lax.rem(i + (by + n), n)

    counter = [0]
    sent = []

    def copy(src, dst, device):
        i = counter[0]
        counter[0] += 1
        return pltpu.make_async_remote_copy(
            src_ref=src, dst_ref=dst, send_sem=send_sem.at[i], recv_sem=recv_sem.at[i],
            device_id=device, device_id_type=MESH,
        )

    def start(*copies):
        for c in copies:
            c.start()
            sent.append(c)
        return copies

    peers = []
    for sd in (-1, 0, 1):
        for sh in (-1, 0, 1):
            if (sd, sh) != (0, 0):
                peers.append({"dev": step(z, sd, 8), "ha": step(y, sh, 4)})
    for k in range(2, 7):
        peers.append({"dev": step(z, k, 8)})
    for k in (-2, -1, 1, 2, 4):
        peers.append({"wa": step(w, k, 8)})
    peers.append({"ha": step(y, 2, 4)})
    barrier = pltpu.get_barrier_semaphore()
    for peer in peers:
        pl.semaphore_signal(barrier, inc=1, device_id=peer, device_id_type=MESH)
    load_u = pltpu.make_async_copy(up_ref, pad_u.at[pl.ds(1, 4), pl.ds(1, 8)], local_sem.at[0])
    load_v = pltpu.make_async_copy(vol_ref, pad_v.at[pl.ds(1, 4), pl.ds(1, 8)], local_sem.at[1])
    load_v.start()
    load_u.start()
    k_copies = [
        pltpu.make_async_copy(k_hbm.at[pl.ds(9 * i, 9)], k_f.at[pl.ds(9 * i, 9)], ksem.at[i])
        for i in range(3)
    ]
    for c in k_copies:
        c.start()
    acc_o[...] = jnp.zeros_like(acc_o)
    acc_g[...] = jnp.zeros_like(acc_g)
    pl.semaphore_wait(barrier, len(peers))

    def send_faces(src, pad):
        copies = []
        for sd in (-1, 0, 1):
            for sh in (-1, 0, 1):
                if (sd, sh) == (0, 0):
                    continue
                d_src, d_dst, d_n = ((0, 5, 1), (0, 1, 4), (3, 0, 1))[sd + 1]
                h_src, h_dst, h_n = ((0, 9, 1), (0, 1, 8), (7, 0, 1))[sh + 1]
                copies.append(copy(
                    src.at[pl.ds(d_src, d_n), pl.ds(h_src, h_n)],
                    pad.at[pl.ds(d_dst, d_n), pl.ds(h_dst, h_n)],
                    {"dev": step(z, sd, 8), "ha": step(y, sh, 4)},
                ))
        return start(*copies)

    def send_columns(pad, col, halo):
        col[0] = pad[:, :, 0:1, :]
        col[1] = pad[:, :, 7:8, :]
        return start(
            copy(col.at[0], halo.at[1], {"wa": step(w, -1, 8)}),
            copy(col.at[1], halo.at[0], {"wa": step(w, 1, 8)}),
        )

    def arrive(copies):
        for c in copies:
            c.wait_recv()

    def windows(pad, halo, hi_ref, lo_ref, shifts):
        def body(d, carry):
            rows = pl.ds(pl.multiple_of(d * 64, 64), 64)
            plane = pad[d]
            at = lax.broadcasted_iota(jnp.int32, plane.shape, 1)
            for c in shifts:
                shifted = plane
                if c != 1:
                    edge = jnp.broadcast_to(halo[c // 2, d], plane.shape)
                    by, row = ((1, 0), None, (7, 7))[c]
                    shifted = jnp.where(at == row, edge, pltpu.roll(plane, by, 1))
                for b in range(3):
                    hi, lo = split(shifted[b : b + 8].reshape(64, plane.shape[-1]))
                    hi_ref[3 * b + c, rows, :] = hi
                    lo_ref[3 * b + c, rows, :] = lo
            return carry

        lax.fori_loop(0, 6, body, 0)

    def window(hi_ref, lo_ref, t):
        rows = pl.ds(pl.multiple_of(lax.div(t, 9) * 64, 64), 256)
        i = lax.rem(t, 9)
        return hi_ref[i, rows, :], lo_ref[i, rows, :]

    def kernel_grad(g):
        def body(i, carry):
            upwin = window(wu_hi, wu_lo, 26 - tap(4 * g + i))
            res = dot3((vt_hi[...], vt_lo[...]), upwin, ((1,), (0,)))
            for block in range(8):
                for half in range(2):
                    part[g, block % 2, block // 2, 2 * i + half] = res[
                        32 * block : 32 * block + 32, 128 * half : 128 * half + 128
                    ]
            return carry

        taps = min(4, 27 - 4 * g)
        lax.fori_loop(0, taps, body, 0)
        for i in range(taps, 4):
            for j in (2 * i, 2 * i + 1):
                part[g, :, :, j] = jnp.zeros((2, 4, 32, 128), F32)
        groups[g].pair()

    def products(first, last):
        def body(t, carry):
            k = split(k_f[t])
            acc_o[...] += dot3(window(wv_hi, wv_lo, t), k, ((1,), (0,)))
            acc_g[...] += dot3(window(wu_hi, wu_lo, 26 - t), k, ((1,), (1,)))
            return carry

        lax.fori_loop(first, last, body, 0)

    def place(axis):
        return {"x": x, "y": y, "z": z}[axis]

    def away(axis, by):
        if axis == "x":
            return {"wa": step(w, 2 * by, 8)}
        return {"ha": step(y, by, 4)} if axis == "y" else {"dev": step(z, by, 8)}

    def direct(axis, chunk, recv):
        n = 8 if axis == "z" else 4
        return start(*(
            copy(chunk(step(place(axis), k, n)), recv.at[k - 1], away(axis, k)) for k in range(1, n)
        ))

    def direct_sum(axis, copies, chunk, recv):
        arrive(copies)
        total = chunk(place(axis))[...]
        for k in range(len(copies)):
            total = total + recv[k]
        return total

    def halves(ref, h):
        if len(ref.shape) == 4:
            return ref.at[:, pl.ds(4 * h, 4)]
        return ref.at[pl.ds(4 * h, 4)]

    def ring_1(axis, chunk, recv):
        far = chunk(step(place(axis), 2, 4))
        return start(
            copy(halves(far, 0), recv.at[0], away(axis, 1)),
            copy(halves(far, 1), recv.at[1], away(axis, -1)),
        )

    def ring_2(axis, copies, chunk, recv, stage, recv_2):
        arrive(copies)
        for h, by in ((0, 1), (1, -1)):
            near = chunk(step(place(axis), by, 4))
            halves(stage.at[h], h)[...] = halves(near, h)[...] + recv[h]
            halves(stage.at[h], 1 - h)[...] = halves(near, 1 - h)[...]
        return start(
            copy(stage.at[0], recv_2.at[0], away(axis, 1)),
            copy(stage.at[1], recv_2.at[1], away(axis, -1)),
        )

    def rows_of(ref, k):
        rows = pl.ds(pl.multiple_of(k * 8, 8), 8)
        return ref.at[(slice(None),) * (len(ref.shape) - 2) + (rows,)]

    class Group:
        def __init__(self, g):
            self.g = g
            self.slot = (g + GROUPS - 1) % GROUPS
            self.sum = summed.at[g]

        def pair(self):
            self.c = start(copy(part.at[self.g, 1 - core], pair.at[self.g], {"wa": w + 1 - 2 * core}))

        def add_pair(self):
            arrive(self.c)
            self.sum[...] = part[self.g, core] + pair[self.g]

    class PlaneGroup(Group):
        def __init__(self, g):
            super().__init__(g)
            self.first = FIRST[g]
            self.second = "y" if self.first == "x" else "x"
            n = FIRST[:g].count(self.first)
            i = 0 if self.first == "x" else 1
            self.r1, self.s2, self.r2 = r1[i].at[n], s2[i].at[n], r2[i].at[n]
            self.mid = mid[i].at[n]
            self.q1 = q1.at[self.slot]
            if self.first == "x":
                self.chunk_1 = lambda k: self.sum.at[k]
                self.chunk_2 = lambda k: rows_of(self.mid, k)
            else:
                self.chunk_1 = lambda k: rows_of(self.sum, k)
                self.chunk_2 = lambda k: self.mid.at[k]

        def e1(self):
            self.add_pair()
            self.c = ring_1(self.first, self.chunk_1, self.r1)

        def e2(self):
            self.c = ring_2(self.first, self.c, self.chunk_1, self.r1, self.s2, self.r2)

        def e3(self):
            self.mid[...] = direct_sum(self.first, self.c, self.chunk_1, self.r2)
            self.c = direct(self.second, self.chunk_2, self.q1)

        def e4(self):
            low[self.slot] = direct_sum(self.second, self.c, self.chunk_2, self.q1)

    class DepthGroup(Group):
        def __init__(self, g):
            super().__init__(g)
            self.chunk_1 = lambda k: self.sum.at[:, k]
            self.chunk_2 = lambda k: zmid.at[k]
            self.chunk_3 = lambda k: rows_of(zlow, k)

        def e1(self):
            self.add_pair()
            self.c = direct("z", self.chunk_1, z1)

        def e2(self):
            zmid[...] = direct_sum("z", self.c, self.chunk_1, z1)
            self.c = direct("x", self.chunk_2, z2)

        def e3(self):
            zlow[...] = direct_sum("x", self.c, self.chunk_2, z2)
            self.c = direct("y", self.chunk_3, z3)

        def result(self):
            return direct_sum("y", self.c, self.chunk_3, z3)

    class Batch:
        def __init__(self, i):
            self.i = i
            lo, hi = BATCHES[i]
            self.n = hi - lo - (1 if hi == GROUPS else 0)
            self.depth_group = hi == GROUPS
            self.lo = lo
            self.sums = pl.ds(lo, self.n)
            self.all = pl.ds(lo, hi - lo)

        def e6(self):
            self.c = start(*(
                copy(low.at[self.sums, step(z, k, 8)], rz.at[k - 1, self.sums], {"dev": step(z, k, 8)})
                for k in range(1, 8)
            ))

        def e7(self):
            arrive(self.c)
            total = low[self.sums, z]
            for k in range(7):
                total = total + rz[k, self.sums]
            fin[self.sums] = total * factor
            if self.depth_group:
                fin[GROUPS - 1] = groups[0].result() * factor
            agz_at = lambda k: agz.at[
                self.all, lax.div(k, 2), :, pl.ds(pl.multiple_of(lax.rem(k, 2) * 128, 128), 128)
            ]
            agz_at(z)[...] = fin[self.all]
            first = counter[0]
            start(*(copy(fin.at[self.all], agz_at(z), {"dev": step(z, k, 8)}) for k in range(1, 8)))
            self.c = [
                self.landed(first + k - 1, agz_at(step(z, -k, 8)), {"dev": step(z, k, 8)})
                for k in range(1, 8)
            ]

        def landed(self, i, slot, device):
            return pltpu.make_async_remote_copy(
                src_ref=slot, dst_ref=slot, send_sem=send_sem.at[i], recv_sem=recv_sem.at[i],
                device_id=device, device_id_type=MESH,
            )

        def e8(self):
            arrive(self.c)
            first = counter[0]
            here = agz.at[self.all]
            there = lambda k: rows_of(kg_ref.at[self.all], k)
            self.local = pltpu.make_async_copy(here, there(y), local_sem.at[4 + self.i])
            self.local.start()
            start(*(copy(here, there(y), {"ha": step(y, k, 4)}) for k in range(1, 4)))
            self.c = [
                self.landed(first + k - 1, there(step(y, -k, 4)), {"ha": step(y, k, 4)})
                for k in range(1, 4)
            ]

        def e9(self):
            self.local.wait()
            arrive(self.c)

    groups = [(DepthGroup if FIRST[g] == "z" else PlaneGroup)(g) for g in range(GROUPS)]
    batches = [Batch(i) for i in range(len(BATCHES))]

    faces_u = send_faces(up_ref, pad_u)
    load_v.wait()
    hi, lo = split(pad_v[1:5, 1:9].reshape(256, 256).T)
    vt_hi[...] = hi
    vt_lo[...] = lo
    load_u.wait()
    arrive(faces_u)
    cols_u = send_columns(pad_u, col_u, halo_u)
    faces_v = send_faces(vol_ref, pad_v)
    windows(pad_u, halo_u, wu_hi, wu_lo, (1,))
    kernel_grad(0)
    kernel_grad(1)
    groups[0].e1()
    arrive(cols_u)
    windows(pad_u, halo_u, wu_hi, wu_lo, (0, 2))
    groups[1].e1()
    kernel_grad(2)
    kernel_grad(3)
    groups[2].e1()
    arrive(faces_v)
    cols_v = send_columns(pad_v, col_v, halo_v)
    kernel_grad(4)
    groups[3].e1()
    groups[1].e2()
    kernel_grad(5)
    groups[4].e1()
    groups[2].e2()
    kernel_grad(6)
    groups[5].e1()
    groups[3].e2()
    windows(pad_v, halo_v, wv_hi, wv_lo, (1,))
    groups[6].e1()
    groups[4].e2()
    arrive(cols_v)
    windows(pad_v, halo_v, wv_hi, wv_lo, (0, 2))
    for c in k_copies:
        c.wait()
    groups[5].e2()
    products(0, 2)
    groups[6].e2()
    groups[1].e3()
    groups[2].e3()
    products(2, 7)
    groups[3].e3()
    groups[4].e3()
    products(7, 11)
    groups[1].e4()
    groups[2].e4()
    products(11, 14)
    groups[5].e3()
    groups[6].e3()
    groups[3].e4()
    groups[4].e4()
    batches[0].e6()
    products(14, 18)
    groups[0].e2()
    groups[5].e4()
    groups[6].e4()
    batches[1].e6()
    products(18, 22)
    batches[0].e7()
    groups[0].e3()
    products(22, 27)
    out_store = pltpu.make_async_copy(acc_o, out_ref, local_sem.at[2])
    vg_store = pltpu.make_async_copy(acc_g, vg_ref, local_sem.at[3])
    out_store.start()
    vg_store.start()
    batches[1].e7()
    batches[0].e8()
    batches[1].e8()
    batches[0].e9()
    batches[1].e9()
    out_store.wait()
    vg_store.wait()
    assert counter[0] == N_SEM, counter[0]
    for c in sent:
        c.wait_send()


def move(out_in, vg_in, kg_in, out_ref, vg_ref, kg_ref, out_v, vg_v, kg_v, sem, sem_2):
    ins = [
        pltpu.make_async_copy(src, dst, sem.at[i])
        for i, (src, dst) in enumerate(((out_in, out_v), (vg_in, vg_v), (kg_in, kg_v)))
    ]
    for c in ins:
        c.start()
    copies = [
        pltpu.make_async_copy(out_v, out_ref, sem_2.at[27]),
        pltpu.make_async_copy(vg_v, vg_ref, sem_2.at[28]),
    ]
    for c, then in zip(ins, copies):
        c.wait()
        then.start()
    ins[2].wait()
    for u in range(27):
        slot = (u // 4 + GROUPS - 1) % GROUPS
        copies.append(pltpu.make_async_copy(kg_v.at[slot, u % 4], kg_ref.at[tap(u)], sem_2.at[u]))
        copies[-1].start()
    for c in copies:
        c.wait()


def per_device(factor, volume, kernel_taps, upstream):
    nx, ny = FIRST.count("x"), FIRST.count("y")
    vmem = pltpu.VMEM
    scratch = [
        vmem((27, 256, 256), F32),
        vmem((6, 10, 8, 256), F32), vmem((6, 10, 8, 256), F32),
        vmem((2, 6, 10, 1, 256), F32), vmem((2, 6, 10, 1, 256), F32),
        vmem((2, 6, 10, 1, 256), F32), vmem((2, 6, 10, 1, 256), F32),
        vmem((9, 384, 256), BF16), vmem((9, 384, 256), BF16),
        vmem((9, 384, 256), BF16), vmem((9, 384, 256), BF16),
        vmem((256, 256), BF16), vmem((256, 256), BF16),
        vmem((256, 256), F32), vmem((256, 256), F32),
        vmem((GROUPS, 2, 4, 8, 32, 128), F32),
        vmem((GROUPS, 4, 8, 32, 128), F32),
        vmem((GROUPS, 4, 8, 32, 128), F32),
        [vmem((nx, 2, 4, 32, 128), F32), vmem((ny, 2, 4, 4, 8, 128), F32)],
        [vmem((nx, 2, 8, 32, 128), F32), vmem((ny, 2, 4, 8, 8, 128), F32)],
        [vmem((nx, 2, 8, 32, 128), F32), vmem((ny, 2, 4, 8, 8, 128), F32)],
        [vmem((nx, 8, 32, 128), F32), vmem((ny, 4, 8, 8, 128), F32)],
        vmem((GROUPS, 3, 8, 8, 128), F32),
        vmem((GROUPS, 8, 8, 128), F32),
        vmem((7, GROUPS, 8, 128), F32),
        vmem((GROUPS, 8, 128), F32),
        vmem((GROUPS, 4, 8, 256), F32),
        vmem((7, 4, 32, 128), F32), vmem((4, 32, 128), F32),
        vmem((3, 32, 128), F32), vmem((32, 128), F32),
        vmem((3, 8, 128), F32),
        pltpu.SemaphoreType.DMA((3,)),
        pltpu.SemaphoreType.DMA((4 + len(BATCHES),)),
        pltpu.SemaphoreType.DMA((N_SEM,)),
        pltpu.SemaphoreType.DMA((N_SEM,)),
    ]
    here = pl.BlockSpec(memory_space=pl.ANY)
    flat = jax.ShapeDtypeStruct((256, 256), F32)
    output, volume_grad, kg = pl.pallas_call(
        functools.partial(kernel, factor),
        out_shape=(flat, flat, jax.ShapeDtypeStruct((GROUPS, 4, 32, 256), F32)),
        in_specs=[here] * 3,
        out_specs=(here,) * 3,
        scratch_shapes=scratch,
        compiler_params=pltpu.CompilerParams(
            collective_id=0, has_side_effects=True, vmem_limit_bytes=56 * 2**20
        ),
    )(volume, upstream, jnp.transpose(kernel_taps, (1, 0, 2)))
    output, volume_grad, kg = pl.pallas_call(
        move,
        out_shape=(flat, flat, jax.ShapeDtypeStruct((27, 32, 256), F32)),
        in_specs=[here] * 3,
        out_specs=(here,) * 3,
        scratch_shapes=[
            vmem((256, 256), F32), vmem((256, 256), F32), vmem((GROUPS, 4, 32, 256), F32),
            pltpu.SemaphoreType.DMA((3,)), pltpu.SemaphoreType.DMA((29,)),
        ],
    )(output, volume_grad, kg)
    return (
        output.reshape(volume.shape),
        volume_grad.reshape(volume.shape),
        jnp.transpose(kg, (1, 0, 2)),
    )


def solution(mesh):
    cells = 256 * mesh.shape["dev"] * mesh.shape["ha"] * mesh.shape["wa"]
    place = P("dev", "ha", "wa", None)
    return jax.shard_map(
        functools.partial(per_device, 1.0 / math.sqrt(cells)),
        mesh=mesh,
        in_specs=(place, P(), place),
        out_specs=(place, place, P("wa", None, None)),
        check_vma=False,
    )
```

time: 88.9 us -> 69.7 us (0.78)
  Pallas kernels: 82.5 us -> 68.8 us
  local copies, waits for them, and re-layouts: 5.52 us -> 0 us
    pallas_call x1 -> x2, Pallas kernels: 82.5 us -> 68.8 us  [the longest x1 66.3 us: per_device(): pl.pallas_call(functools.partial(kernel, factor), out_shape=(flat, flat,...]
    unnamed x3 -> x0, local copies, waits for them, and re-layouts: 5.52 us -> none
where the time goes in v2:
time: 69.7 us; the launch traced here: 69.5 us
  Pallas kernels  68.8 us (99%)
    pallas_call x1, Pallas kernels, per_device(): pl.pallas_call(functools.partial(kernel, factor), out_shape=(flat, flat,...  66.3 us
    pallas_call x1, Pallas kernels, per_device(): pl.pallas_call(move, out_shape=(flat, flat, jax.ShapeDtypeStruct((27, 32,...  2.52 us

profile of v2, /device:TPU:2, one launch (start us, length us, event | category | flops | bytes accessed | tf_op | source)
XLA Modules:
  0.0 69.5 jit_solution(16847871204579510764)
XLA Ops:
  0.6 66.3 %shard_map.58 = (f32[256,256]{1,0:T(8,128)}, f32[256,256]{1,0:T(8,128)}, f32[7,4,32,256]{3,2,1,0:T(8,128)}) custom-call(f32[4,8,8,256]{3,2,1,0:T(8,128)} %vol_ref.1, f32[4,8,8,256]{3,2,1,0:T(8,128)} %up_ref.1, f32[27,256,256]{2,1,0:T(8,128)} %bitcast.4), custom_call_target="tpu_custom_call" | custom-call | tf_op jit(solution)/shard_map/pallas_call | solution.py:490
  66.9 2.5 %shard_map.59 = (f32[256,256]{1,0:T(8,128)}, f32[256,256]{1,0:T(8,128)}, f32[27,32,256]{2,1,0:T(8,128)}) custom-call(f32[256,256]{1,0:T(8,128)} %get-tuple-element.9.out_in, f32[256,256]{1,0:T(8,128)} %get-tuple-element.10.vg_in, f32[7,4,32,256]{3,2,1,0:T(8,128)} %get-tuple-element.11.kg_in), custom_call_target="tpu_custom_call" | custom-call | tf_op jit(solution)/shard_map/pallas_call | solution.py:500

commit v3 on v2

--- a/solution.py
+++ b/solution.py
@@ -13,16 +13,17 @@
 BF16 = jnp.bfloat16
 
 GROUPS = 7
-FIRST = ("z", "x", "y", "x", "y", "x", "y")
-BATCHES = ((0, 4), (4, 7))
-N_SEM = 2 * 10 + GROUPS + 6 * (2 + 2 + 3) + (7 + 3 + 3) + len(BATCHES) * (7 + 7 + 3)
+FIRST = ("x", "y", "z", "x", "y", "x", "y")
+DEPTH = FIRST.index("z")
+SLOT = (0, 1, 6, 2, 3, 4, 5)
+BATCHES = ((0, 2), (2, 4), (4, 7))
+N_SEM = 2 * 26 + GROUPS + 6 * (2 + 2 + 3) + (7 + 3 + 3) + len(BATCHES) * (7 + 7 + 3)
 
 
 def tap(u):
     if isinstance(u, int):
-        return 3 * u + 1 if u < 9 else 3 * ((u - 9) // 2) + 2 * ((u - 9) % 2)
-    v = jnp.maximum(u - 9, 0)
-    return jnp.where(u < 9, 3 * u + 1, 3 * lax.div(v, 2) + 2 * lax.rem(v, 2))
+        return u + 9 if u < 9 else u - 9 if u < 18 else u
+    return jnp.where(u < 9, u + 9, jnp.where(u < 18, u - 9, u))
 
 
 def split(x):
@@ -71,23 +72,31 @@
             sent.append(c)
         return copies
 
-    peers = []
-    for sd in (-1, 0, 1):
-        for sh in (-1, 0, 1):
-            if (sd, sh) != (0, 0):
-                peers.append({"dev": step(z, sd, 8), "ha": step(y, sh, 4)})
+    around = [
+        (sd, sh, sw) for sd in (0, -1, 1) for sh in (-1, 0, 1) for sw in (-1, 0, 1)
+        if (sd, sh, sw) != (0, 0, 0)
+    ]
+
+    def neighbour(sd, sh, sw):
+        return {"dev": step(z, sd, 8), "ha": step(y, sh, 4), "wa": step(w, sw, 8)}
+
+    peers = [neighbour(*by) for by in around]
     for k in range(2, 7):
         peers.append({"dev": step(z, k, 8)})
-    for k in (-2, -1, 1, 2, 4):
+    for k in (-2, 2, 4):
         peers.append({"wa": step(w, k, 8)})
     peers.append({"ha": step(y, 2, 4)})
     barrier = pltpu.get_barrier_semaphore()
     for peer in peers:
         pl.semaphore_signal(barrier, inc=1, device_id=peer, device_id_type=MESH)
+    def cut_columns(pad, col):
+        col[0] = pad[1:5, 1:9, 7:8, :]
+        col[1] = pad[1:5, 1:9, 0:1, :]
+
     load_u = pltpu.make_async_copy(up_ref, pad_u.at[pl.ds(1, 4), pl.ds(1, 8)], local_sem.at[0])
     load_v = pltpu.make_async_copy(vol_ref, pad_v.at[pl.ds(1, 4), pl.ds(1, 8)], local_sem.at[1])
+    load_u.start()
     load_v.start()
-    load_u.start()
     k_copies = [
         pltpu.make_async_copy(k_hbm.at[pl.ds(9 * i, 9)], k_f.at[pl.ds(9 * i, 9)], ksem.at[i])
         for i in range(3)
@@ -96,53 +105,55 @@
         c.start()
     acc_o[...] = jnp.zeros_like(acc_o)
     acc_g[...] = jnp.zeros_like(acc_g)
+    load_u.wait()
+    cut_columns(pad_u, col_u)
+    load_v.wait()
+    cut_columns(pad_v, col_v)
+    hi, lo = split(pad_v[1:5, 1:9].reshape(256, 256).T)
+    vt_hi[...] = hi
+    vt_lo[...] = lo
     pl.semaphore_wait(barrier, len(peers))
 
-    def send_faces(src, pad):
+    def send_halo(src, pad, col, halo, pieces):
         copies = []
-        for sd in (-1, 0, 1):
-            for sh in (-1, 0, 1):
-                if (sd, sh) == (0, 0):
-                    continue
-                d_src, d_dst, d_n = ((0, 5, 1), (0, 1, 4), (3, 0, 1))[sd + 1]
-                h_src, h_dst, h_n = ((0, 9, 1), (0, 1, 8), (7, 0, 1))[sh + 1]
-                copies.append(copy(
-                    src.at[pl.ds(d_src, d_n), pl.ds(h_src, h_n)],
-                    pad.at[pl.ds(d_dst, d_n), pl.ds(h_dst, h_n)],
-                    {"dev": step(z, sd, 8), "ha": step(y, sh, 4)},
-                ))
+        for sd, sh, sw in pieces:
+            d_src, d_dst, d_n = ((0, 5, 1), (0, 1, 4), (3, 0, 1))[sd + 1]
+            h_src, h_dst, h_n = ((0, 9, 1), (0, 1, 8), (7, 0, 1))[sh + 1]
+            at = (pl.ds(d_src, d_n), pl.ds(h_src, h_n))
+            to = (pl.ds(d_dst, d_n), pl.ds(h_dst, h_n))
+            if sw == 0:
+                a, b = src.at[at], pad.at[to]
+            else:
+                side = 0 if sw == 1 else 1
+                a, b = col.at[(side,) + at], halo.at[(side,) + to]
+            copies.append(copy(a, b, neighbour(sd, sh, sw)))
         return start(*copies)
-
-    def send_columns(pad, col, halo):
-        col[0] = pad[:, :, 0:1, :]
-        col[1] = pad[:, :, 7:8, :]
-        return start(
-            copy(col.at[0], halo.at[1], {"wa": step(w, -1, 8)}),
-            copy(col.at[1], halo.at[0], {"wa": step(w, 1, 8)}),
-        )
 
     def arrive(copies):
         for c in copies:
             c.wait_recv()
 
-    def windows(pad, halo, hi_ref, lo_ref, shifts):
-        def body(d, carry):
+    def windows(pad, halo, hi_ref, lo_ref, planes):
+        def body(i, carry):
+            d = planes.start + i * planes.step
             rows = pl.ds(pl.multiple_of(d * 64, 64), 64)
             plane = pad[d]
             at = lax.broadcasted_iota(jnp.int32, plane.shape, 1)
-            for c in shifts:
-                shifted = plane
-                if c != 1:
-                    edge = jnp.broadcast_to(halo[c // 2, d], plane.shape)
-                    by, row = ((1, 0), None, (7, 7))[c]
-                    shifted = jnp.where(at == row, edge, pltpu.roll(plane, by, 1))
-                for b in range(3):
-                    hi, lo = split(shifted[b : b + 8].reshape(64, plane.shape[-1]))
+            before = jnp.broadcast_to(halo[0, d], plane.shape)
+            after = jnp.broadcast_to(halo[1, d], plane.shape)
+            shifted = (
+                jnp.where(at == 0, before, pltpu.roll(plane, 1, 1)),
+                plane,
+                jnp.where(at == 7, after, pltpu.roll(plane, 7, 1)),
+            )
+            for b in range(3):
+                for c in range(3):
+                    hi, lo = split(shifted[c][b : b + 8].reshape(64, plane.shape[-1]))
                     hi_ref[3 * b + c, rows, :] = hi
                     lo_ref[3 * b + c, rows, :] = lo
             return carry
 
-        lax.fori_loop(0, 6, body, 0)
+        lax.fori_loop(0, len(planes), body, 0)
 
     def window(hi_ref, lo_ref, t):
         rows = pl.ds(pl.multiple_of(lax.div(t, 9) * 64, 64), 256)
@@ -227,7 +238,7 @@
     class Group:
         def __init__(self, g):
             self.g = g
-            self.slot = (g + GROUPS - 1) % GROUPS
+            self.slot = SLOT[g]
             self.sum = summed.at[g]
 
         def pair(self):
@@ -313,7 +324,7 @@
                 total = total + rz[k, self.sums]
             fin[self.sums] = total * factor
             if self.depth_group:
-                fin[GROUPS - 1] = groups[0].result() * factor
+                fin[GROUPS - 1] = groups[DEPTH].result() * factor
             agz_at = lambda k: agz.at[
                 self.all, lax.div(k, 2), :, pl.ds(pl.multiple_of(lax.rem(k, 2) * 128, 128), 128)
             ]
@@ -351,78 +362,72 @@
     groups = [(DepthGroup if FIRST[g] == "z" else PlaneGroup)(g) for g in range(GROUPS)]
     batches = [Batch(i) for i in range(len(BATCHES))]
 
-    faces_u = send_faces(up_ref, pad_u)
-    load_v.wait()
-    hi, lo = split(pad_v[1:5, 1:9].reshape(256, 256).T)
-    vt_hi[...] = hi
-    vt_lo[...] = lo
-    load_u.wait()
-    arrive(faces_u)
-    cols_u = send_columns(pad_u, col_u, halo_u)
-    faces_v = send_faces(vol_ref, pad_v)
-    windows(pad_u, halo_u, wu_hi, wu_lo, (1,))
+    flat_u = send_halo(up_ref, pad_u, col_u, halo_u, around[:8])
+    deep_u = send_halo(up_ref, pad_u, col_u, halo_u, around[8:])
+    arrive(flat_u)
+    windows(pad_u, halo_u, wu_hi, wu_lo, range(1, 5))
     kernel_grad(0)
     kernel_grad(1)
+    arrive(deep_u)
+    windows(pad_u, halo_u, wu_hi, wu_lo, range(0, 6, 5))
     groups[0].e1()
-    arrive(cols_u)
-    windows(pad_u, halo_u, wu_hi, wu_lo, (0, 2))
+    kernel_grad(2)
     groups[1].e1()
-    kernel_grad(2)
+    halos_v = send_halo(vol_ref, pad_v, col_v, halo_v, around)
     kernel_grad(3)
     groups[2].e1()
-    arrive(faces_v)
-    cols_v = send_columns(pad_v, col_v, halo_v)
     kernel_grad(4)
     groups[3].e1()
-    groups[1].e2()
+    groups[0].e2()
     kernel_grad(5)
     groups[4].e1()
-    groups[2].e2()
+    groups[1].e2()
     kernel_grad(6)
     groups[5].e1()
     groups[3].e2()
-    windows(pad_v, halo_v, wv_hi, wv_lo, (1,))
     groups[6].e1()
     groups[4].e2()
-    arrive(cols_v)
-    windows(pad_v, halo_v, wv_hi, wv_lo, (0, 2))
+    arrive(halos_v)
+    windows(pad_v, halo_v, wv_hi, wv_lo, range(6))
     for c in k_copies:
         c.wait()
     groups[5].e2()
-    products(0, 2)
     groups[6].e2()
+    products(0, 1)
+    groups[0].e3()
     groups[1].e3()
-    groups[2].e3()
-    products(2, 7)
+    products(1, 6)
     groups[3].e3()
     groups[4].e3()
-    products(7, 11)
+    groups[0].e4()
     groups[1].e4()
-    groups[2].e4()
-    products(11, 14)
+    batches[0].e6()
+    products(6, 11)
     groups[5].e3()
     groups[6].e3()
     groups[3].e4()
     groups[4].e4()
-    batches[0].e6()
-    products(14, 18)
-    groups[0].e2()
+    batches[1].e6()
+    products(11, 16)
+    groups[2].e2()
+    batches[0].e7()
     groups[5].e4()
     groups[6].e4()
-    batches[1].e6()
-    products(18, 22)
-    batches[0].e7()
-    groups[0].e3()
+    batches[2].e6()
+    products(16, 22)
+    groups[2].e3()
+    batches[1].e7()
+    batches[0].e8()
     products(22, 27)
     out_store = pltpu.make_async_copy(acc_o, out_ref, local_sem.at[2])
     vg_store = pltpu.make_async_copy(acc_g, vg_ref, local_sem.at[3])
     out_store.start()
     vg_store.start()
-    batches[1].e7()
-    batches[0].e8()
+    batches[2].e7()
     batches[1].e8()
-    batches[0].e9()
-    batches[1].e9()
+    batches[2].e8()
+    for batch in batches:
+        batch.e9()
     out_store.wait()
     vg_store.wait()
     assert counter[0] == N_SEM, counter[0]
@@ -446,7 +451,7 @@
         then.start()
     ins[2].wait()
     for u in range(27):
-        slot = (u // 4 + GROUPS - 1) % GROUPS
+        slot = SLOT[u // 4]
         copies.append(pltpu.make_async_copy(kg_v.at[slot, u % 4], kg_ref.at[tap(u)], sem_2.at[u]))
         copies[-1].start()
     for c in copies:
@@ -459,7 +464,7 @@
     scratch = [
         vmem((27, 256, 256), F32),
         vmem((6, 10, 8, 256), F32), vmem((6, 10, 8, 256), F32),
-        vmem((2, 6, 10, 1, 256), F32), vmem((2, 6, 10, 1, 256), F32),
+        vmem((2, 4, 8, 1, 256), F32), vmem((2, 4, 8, 1, 256), F32),
         vmem((2, 6, 10, 1, 256), F32), vmem((2, 6, 10, 1, 256), F32),
         vmem((9, 384, 256), BF16), vmem((9, 384, 256), BF16),
         vmem((9, 384, 256), BF16), vmem((9, 384, 256), BF16),

time: 69.7 us -> 66.8 us (0.958)
  Pallas kernels: 68.8 us -> 66 us
    pallas_call x1, Pallas kernels: 66.3 us -> 63.5 us  [per_device(): pl.pallas_call(functools.partial(kernel, factor), out_shape=(flat, flat,...]
where the time goes in v3:
time: 66.8 us; the launch traced here: 66.7 us
  Pallas kernels  66 us (99%)
    pallas_call x1, Pallas kernels, per_device(): pl.pallas_call(functools.partial(kernel, factor), out_shape=(flat, flat,...  63.5 us
    pallas_call x1, Pallas kernels, per_device(): pl.pallas_call(move, out_shape=(flat, flat, jax.ShapeDtypeStruct((27, 32,...  2.52 us

profile of v3, /device:TPU:2, one launch (start us, length us, event | category | flops | bytes accessed | tf_op | source)
XLA Modules:
  0.0 66.7 jit_solution(10748883999796434894)
XLA Ops:
  0.6 63.5 %shard_map.58 = (f32[256,256]{1,0:T(8,128)}, f32[256,256]{1,0:T(8,128)}, f32[7,4,32,256]{3,2,1,0:T(8,128)}) custom-call(f32[4,8,8,256]{3,2,1,0:T(8,128)} %vol_ref.1, f32[4,8,8,256]{3,2,1,0:T(8,128)} %up_ref.1, f32[27,256,256]{2,1,0:T(8,128)} %bitcast.4), custom_call_target="tpu_custom_call" | custom-call | tf_op jit(solution)/shard_map/pallas_call | solution.py:495
  64.2 2.5 %shard_map.59 = (f32[256,256]{1,0:T(8,128)}, f32[256,256]{1,0:T(8,128)}, f32[27,32,256]{2,1,0:T(8,128)}) custom-call(f32[256,256]{1,0:T(8,128)} %get-tuple-element.9.out_in, f32[256,256]{1,0:T(8,128)} %get-tuple-element.10.vg_in, f32[7,4,32,256]{3,2,1,0:T(8,128)} %get-tuple-element.11.kg_in), custom_call_target="tpu_custom_call" | custom-call | tf_op jit(solution)/shard_map/pallas_call | solution.py:505

commit v4 on v3

--- a/solution.py
+++ b/solution.py
@@ -15,15 +15,13 @@
 GROUPS = 7
 FIRST = ("x", "y", "z", "x", "y", "x", "y")
 DEPTH = FIRST.index("z")
-SLOT = (0, 1, 6, 2, 3, 4, 5)
-BATCHES = ((0, 2), (2, 4), (4, 7))
-N_SEM = 2 * 26 + GROUPS + 6 * (2 + 2 + 3) + (7 + 3 + 3) + len(BATCHES) * (7 + 7 + 3)
+SLOT = (0, 1, 4, 2, 3, 5, 6)
+BATCHES = ((0, 2), (2, 5), (5, 7))
+N_SEM = 2 * 26 + GROUPS + 6 * (4 + 2 + 3) + (7 + 3 + 3) + len(BATCHES) * (7 + 7 + 3)
 
 
 def tap(u):
-    if isinstance(u, int):
-        return u + 9 if u < 9 else u - 9 if u < 18 else u
-    return jnp.where(u < 9, u + 9, jnp.where(u < 18, u - 9, u))
+    return u + 9 if u < 9 else u - 9 if u < 18 else u
 
 
 def split(x):
@@ -43,8 +41,8 @@
     factor,
     vol_ref, up_ref, k_hbm, out_ref, vg_ref, kg_ref,
     k_f, pad_v, pad_u, col_v, col_u, halo_v, halo_u,
-    wv_hi, wv_lo, wu_hi, wu_lo, vt_hi, vt_lo, acc_o, acc_g,
-    part, pair, summed, r1, s2, r2, mid, q1, low, rz, fin, agz,
+    wv_hi, wv_lo, wu_hi, wu_lo, vt_hi, vt_lo,
+    part, pair, summed, r1, s2, r2, mid, q1, low, rz, fin, agz, gathered,
     z1, zmid, z2, zlow, z3,
     ksem, local_sem, send_sem, recv_sem,
 ):
@@ -72,6 +70,10 @@
             sent.append(c)
         return copies
 
+    load_u = pltpu.make_async_copy(up_ref, pad_u.at[pl.ds(1, 4), pl.ds(1, 8)], local_sem.at[0])
+    load_v = pltpu.make_async_copy(vol_ref, pad_v.at[pl.ds(1, 4), pl.ds(1, 8)], local_sem.at[1])
+    load_u.start()
+    load_v.start()
     around = [
         (sd, sh, sw) for sd in (0, -1, 1) for sh in (-1, 0, 1) for sw in (-1, 0, 1)
         if (sd, sh, sw) != (0, 0, 0)
@@ -93,25 +95,10 @@
         col[0] = pad[1:5, 1:9, 7:8, :]
         col[1] = pad[1:5, 1:9, 0:1, :]
 
-    load_u = pltpu.make_async_copy(up_ref, pad_u.at[pl.ds(1, 4), pl.ds(1, 8)], local_sem.at[0])
-    load_v = pltpu.make_async_copy(vol_ref, pad_v.at[pl.ds(1, 4), pl.ds(1, 8)], local_sem.at[1])
-    load_u.start()
-    load_v.start()
     k_copies = [
         pltpu.make_async_copy(k_hbm.at[pl.ds(9 * i, 9)], k_f.at[pl.ds(9 * i, 9)], ksem.at[i])
         for i in range(3)
     ]
-    for c in k_copies:
-        c.start()
-    acc_o[...] = jnp.zeros_like(acc_o)
-    acc_g[...] = jnp.zeros_like(acc_g)
-    load_u.wait()
-    cut_columns(pad_u, col_u)
-    load_v.wait()
-    cut_columns(pad_v, col_v)
-    hi, lo = split(pad_v[1:5, 1:9].reshape(256, 256).T)
-    vt_hi[...] = hi
-    vt_lo[...] = lo
     pl.semaphore_wait(barrier, len(peers))
 
     def send_halo(src, pad, col, halo, pieces):
@@ -156,36 +143,45 @@
         lax.fori_loop(0, len(planes), body, 0)
 
     def window(hi_ref, lo_ref, t):
+        t = jnp.int32(t)
         rows = pl.ds(pl.multiple_of(lax.div(t, 9) * 64, 64), 256)
         i = lax.rem(t, 9)
         return hi_ref[i, rows, :], lo_ref[i, rows, :]
 
     def kernel_grad(g):
-        def body(i, carry):
-            upwin = window(wu_hi, wu_lo, 26 - tap(4 * g + i))
+        taps = min(4, 27 - 4 * g)
+        for i in range(taps):
+            d, at = divmod(26 - tap(4 * g + i), 9)
+            rows = slice(64 * d, 64 * d + 256)
+            upwin = wu_hi[at, rows, :], wu_lo[at, rows, :]
             res = dot3((vt_hi[...], vt_lo[...]), upwin, ((1,), (0,)))
             for block in range(8):
                 for half in range(2):
                     part[g, block % 2, block // 2, 2 * i + half] = res[
                         32 * block : 32 * block + 32, 128 * half : 128 * half + 128
                     ]
-            return carry
-
-        taps = min(4, 27 - 4 * g)
-        lax.fori_loop(0, taps, body, 0)
         for i in range(taps, 4):
             for j in (2 * i, 2 * i + 1):
                 part[g, :, :, j] = jnp.zeros((2, 4, 32, 128), F32)
         groups[g].pair()
 
     def products(first, last):
-        def body(t, carry):
-            k = split(k_f[t])
-            acc_o[...] += dot3(window(wv_hi, wv_lo, t), k, ((1,), (0,)))
-            acc_g[...] += dot3(window(wu_hi, wu_lo, 26 - t), k, ((1,), (1,)))
+        def add(taps):
+            out, grad = 0.0, 0.0
+            for t in taps:
+                k = split(k_f[t])
+                out += dot3(window(wv_hi, wv_lo, t), k, ((1,), (0,)))
+                grad += dot3(window(wu_hi, wu_lo, 26 - t), k, ((1,), (1,)))
+            out_ref[...] += out
+            vg_ref[...] += grad
+
+        def body(i, carry):
+            add((first + 2 * i, first + 2 * i + 1))
             return carry
 
-        lax.fori_loop(first, last, body, 0)
+        lax.fori_loop(0, (last - first) // 2, body, 0)
+        if (last - first) % 2:
+            add((last - 1,))
 
     def place(axis):
         return {"x": x, "y": y, "z": z}[axis]
@@ -213,22 +209,24 @@
             return ref.at[:, pl.ds(4 * h, 4)]
         return ref.at[pl.ds(4 * h, 4)]
 
-    def ring_1(axis, chunk, recv):
-        far = chunk(step(place(axis), 2, 4))
+    def ring_1(axis, chunk, recv, recv_2):
+        i = place(axis)
+        far, above, below = (chunk(step(i, k, 4)) for k in (2, 1, -1))
         return start(
             copy(halves(far, 0), recv.at[0], away(axis, 1)),
             copy(halves(far, 1), recv.at[1], away(axis, -1)),
+        ), start(
+            copy(halves(above, 1), halves(recv_2.at[0], 1), away(axis, 1)),
+            copy(halves(below, 0), halves(recv_2.at[1], 0), away(axis, -1)),
         )
 
     def ring_2(axis, copies, chunk, recv, stage, recv_2):
         arrive(copies)
         for h, by in ((0, 1), (1, -1)):
-            near = chunk(step(place(axis), by, 4))
-            halves(stage.at[h], h)[...] = halves(near, h)[...] + recv[h]
-            halves(stage.at[h], 1 - h)[...] = halves(near, 1 - h)[...]
+            stage[h] = halves(chunk(step(place(axis), by, 4)), h)[...] + recv[h]
         return start(
-            copy(stage.at[0], recv_2.at[0], away(axis, 1)),
-            copy(stage.at[1], recv_2.at[1], away(axis, -1)),
+            copy(stage.at[0], halves(recv_2.at[0], 0), away(axis, 1)),
+            copy(stage.at[1], halves(recv_2.at[1], 1), away(axis, -1)),
         )
 
     def rows_of(ref, k):
@@ -267,12 +265,13 @@
 
         def e1(self):
             self.add_pair()
-            self.c = ring_1(self.first, self.chunk_1, self.r1)
+            self.c, self.near = ring_1(self.first, self.chunk_1, self.r1, self.r2)
 
         def e2(self):
             self.c = ring_2(self.first, self.c, self.chunk_1, self.r1, self.s2, self.r2)
 
         def e3(self):
+            arrive(self.near)
             self.mid[...] = direct_sum(self.first, self.c, self.chunk_1, self.r2)
             self.c = direct(self.second, self.chunk_2, self.q1)
 
@@ -305,8 +304,8 @@
         def __init__(self, i):
             self.i = i
             lo, hi = BATCHES[i]
-            self.n = hi - lo - (1 if hi == GROUPS else 0)
-            self.depth_group = hi == GROUPS
+            self.depth_group = hi == SLOT[DEPTH] + 1
+            self.n = hi - lo - (1 if self.depth_group else 0)
             self.lo = lo
             self.sums = pl.ds(lo, self.n)
             self.all = pl.ds(lo, hi - lo)
@@ -324,7 +323,7 @@
                 total = total + rz[k, self.sums]
             fin[self.sums] = total * factor
             if self.depth_group:
-                fin[GROUPS - 1] = groups[DEPTH].result() * factor
+                fin[SLOT[DEPTH]] = groups[DEPTH].result() * factor
             agz_at = lambda k: agz.at[
                 self.all, lax.div(k, 2), :, pl.ds(pl.multiple_of(lax.rem(k, 2) * 128, 128), 128)
             ]
@@ -346,9 +345,8 @@
             arrive(self.c)
             first = counter[0]
             here = agz.at[self.all]
-            there = lambda k: rows_of(kg_ref.at[self.all], k)
-            self.local = pltpu.make_async_copy(here, there(y), local_sem.at[4 + self.i])
-            self.local.start()
+            there = lambda k: rows_of(gathered.at[self.all], k)
+            there(y)[...] = agz[self.all]
             start(*(copy(here, there(y), {"ha": step(y, k, 4)}) for k in range(1, 4)))
             self.c = [
                 self.landed(first + k - 1, there(step(y, -k, 4)), {"ha": step(y, k, 4)})
@@ -356,104 +354,103 @@
             ]
 
         def e9(self):
-            self.local.wait()
             arrive(self.c)
+            for u in range(27):
+                if BATCHES[self.i][0] <= SLOT[u // 4] < BATCHES[self.i][1]:
+                    kg_ref[tap(u)] = gathered[SLOT[u // 4], u % 4]
 
     groups = [(DepthGroup if FIRST[g] == "z" else PlaneGroup)(g) for g in range(GROUPS)]
     batches = [Batch(i) for i in range(len(BATCHES))]
 
-    flat_u = send_halo(up_ref, pad_u, col_u, halo_u, around[:8])
-    deep_u = send_halo(up_ref, pad_u, col_u, halo_u, around[8:])
+    inner = [by for by in around if by[2] == 0]
+    outer = [by for by in around if by[2] != 0]
+    flat_u = send_halo(up_ref, pad_u, col_u, halo_u, inner[:2])
+    deep_u = send_halo(up_ref, pad_u, col_u, halo_u, inner[2:])
+    load_u.wait()
+    cut_columns(pad_u, col_u)
+    flat_u += send_halo(up_ref, pad_u, col_u, halo_u, outer[:6])
+    deep_u += send_halo(up_ref, pad_u, col_u, halo_u, outer[6:])
+    for c in k_copies:
+        c.start()
+    load_v.wait()
+    cut_columns(pad_v, col_v)
+    hi, lo = split(pad_v[1:5, 1:9].reshape(256, 256).T)
+    vt_hi[...] = hi
+    vt_lo[...] = lo
+    out_ref[...] = jnp.zeros_like(out_ref)
+    vg_ref[...] = jnp.zeros_like(vg_ref)
     arrive(flat_u)
+    halos_v = send_halo(vol_ref, pad_v, col_v, halo_v, around)
     windows(pad_u, halo_u, wu_hi, wu_lo, range(1, 5))
     kernel_grad(0)
     kernel_grad(1)
     arrive(deep_u)
     windows(pad_u, halo_u, wu_hi, wu_lo, range(0, 6, 5))
+    kernel_grad(2)
     groups[0].e1()
-    kernel_grad(2)
+    kernel_grad(3)
     groups[1].e1()
-    halos_v = send_halo(vol_ref, pad_v, col_v, halo_v, around)
-    kernel_grad(3)
+    kernel_grad(4)
     groups[2].e1()
-    kernel_grad(4)
     groups[3].e1()
-    groups[0].e2()
     kernel_grad(5)
     groups[4].e1()
-    groups[1].e2()
     kernel_grad(6)
     groups[5].e1()
+    groups[6].e1()
+    groups[0].e2()
+    groups[1].e2()
     groups[3].e2()
-    groups[6].e1()
     groups[4].e2()
     arrive(halos_v)
     windows(pad_v, halo_v, wv_hi, wv_lo, range(6))
+    groups[5].e2()
+    groups[6].e2()
     for c in k_copies:
         c.wait()
-    groups[5].e2()
-    groups[6].e2()
-    products(0, 1)
+    products(0, 8)
     groups[0].e3()
     groups[1].e3()
-    products(1, 6)
+    products(8, 14)
     groups[3].e3()
     groups[4].e3()
+    products(14, 18)
     groups[0].e4()
     groups[1].e4()
     batches[0].e6()
-    products(6, 11)
+    products(18, 22)
     groups[5].e3()
     groups[6].e3()
+    groups[2].e2()
+    products(22, 24)
     groups[3].e4()
     groups[4].e4()
     batches[1].e6()
-    products(11, 16)
-    groups[2].e2()
+    products(24, 27)
+    groups[2].e3()
     batches[0].e7()
     groups[5].e4()
     groups[6].e4()
     batches[2].e6()
-    products(16, 22)
-    groups[2].e3()
     batches[1].e7()
     batches[0].e8()
-    products(22, 27)
-    out_store = pltpu.make_async_copy(acc_o, out_ref, local_sem.at[2])
-    vg_store = pltpu.make_async_copy(acc_g, vg_ref, local_sem.at[3])
-    out_store.start()
-    vg_store.start()
     batches[2].e7()
     batches[1].e8()
     batches[2].e8()
     for batch in batches:
         batch.e9()
-    out_store.wait()
-    vg_store.wait()
     assert counter[0] == N_SEM, counter[0]
     for c in sent:
         c.wait_send()
 
 
-def move(out_in, vg_in, kg_in, out_ref, vg_ref, kg_ref, out_v, vg_v, kg_v, sem, sem_2):
-    ins = [
+def store(out_in, vg_in, kg_in, out_ref, vg_ref, kg_ref, sem):
+    copies = [
         pltpu.make_async_copy(src, dst, sem.at[i])
-        for i, (src, dst) in enumerate(((out_in, out_v), (vg_in, vg_v), (kg_in, kg_v)))
+        for i, (src, dst) in enumerate(((kg_in, kg_ref), (out_in, out_ref), (vg_in, vg_ref)))
     ]
-    for c in ins:
+    for c in copies:
         c.start()
-    copies = [
-        pltpu.make_async_copy(out_v, out_ref, sem_2.at[27]),
-        pltpu.make_async_copy(vg_v, vg_ref, sem_2.at[28]),
-    ]
-    for c, then in zip(ins, copies):
-        c.wait()
-        then.start()
-    ins[2].wait()
-    for u in range(27):
-        slot = SLOT[u // 4]
-        copies.append(pltpu.make_async_copy(kg_v.at[slot, u % 4], kg_ref.at[tap(u)], sem_2.at[u]))
-        copies[-1].start()
     for c in copies:
         c.wait()
 
@@ -469,12 +466,11 @@
         vmem((9, 384, 256), BF16), vmem((9, 384, 256), BF16),
         vmem((9, 384, 256), BF16), vmem((9, 384, 256), BF16),
         vmem((256, 256), BF16), vmem((256, 256), BF16),
-        vmem((256, 256), F32), vmem((256, 256), F32),
         vmem((GROUPS, 2, 4, 8, 32, 128), F32),
         vmem((GROUPS, 4, 8, 32, 128), F32),
         vmem((GROUPS, 4, 8, 32, 128), F32),
         [vmem((nx, 2, 4, 32, 128), F32), vmem((ny, 2, 4, 4, 8, 128), F32)],
-        [vmem((nx, 2, 8, 32, 128), F32), vmem((ny, 2, 4, 8, 8, 128), F32)],
+        [vmem((nx, 2, 4, 32, 128), F32), vmem((ny, 2, 4, 4, 8, 128), F32)],
         [vmem((nx, 2, 8, 32, 128), F32), vmem((ny, 2, 4, 8, 8, 128), F32)],
         [vmem((nx, 8, 32, 128), F32), vmem((ny, 4, 8, 8, 128), F32)],
         vmem((GROUPS, 3, 8, 8, 128), F32),
@@ -482,36 +478,37 @@
         vmem((7, GROUPS, 8, 128), F32),
         vmem((GROUPS, 8, 128), F32),
         vmem((GROUPS, 4, 8, 256), F32),
+        vmem((GROUPS, 4, 32, 256), F32),
         vmem((7, 4, 32, 128), F32), vmem((4, 32, 128), F32),
         vmem((3, 32, 128), F32), vmem((32, 128), F32),
         vmem((3, 8, 128), F32),
         pltpu.SemaphoreType.DMA((3,)),
-        pltpu.SemaphoreType.DMA((4 + len(BATCHES),)),
+        pltpu.SemaphoreType.DMA((2,)),
         pltpu.SemaphoreType.DMA((N_SEM,)),
         pltpu.SemaphoreType.DMA((N_SEM,)),
     ]
     here = pl.BlockSpec(memory_space=pl.ANY)
-    flat = jax.ShapeDtypeStruct((256, 256), F32)
+    held = pl.BlockSpec(memory_space=pltpu.VMEM)
     output, volume_grad, kg = pl.pallas_call(
         functools.partial(kernel, factor),
-        out_shape=(flat, flat, jax.ShapeDtypeStruct((GROUPS, 4, 32, 256), F32)),
+        out_shape=(vmem((256, 256), F32), vmem((256, 256), F32), vmem((27, 32, 256), F32)),
         in_specs=[here] * 3,
-        out_specs=(here,) * 3,
+        out_specs=(held,) * 3,
         scratch_shapes=scratch,
         compiler_params=pltpu.CompilerParams(
             collective_id=0, has_side_effects=True, vmem_limit_bytes=56 * 2**20
         ),
     )(volume, upstream, jnp.transpose(kernel_taps, (1, 0, 2)))
+    results = [
+        pltpu.with_memory_space_constraint(r, pltpu.VMEM) for r in (output, volume_grad, kg)
+    ]
     output, volume_grad, kg = pl.pallas_call(
-        move,
-        out_shape=(flat, flat, jax.ShapeDtypeStruct((27, 32, 256), F32)),
-        in_specs=[here] * 3,
+        store,
+        out_shape=tuple(jax.ShapeDtypeStruct(r.shape, F32) for r in results),
+        in_specs=[held] * 3,
         out_specs=(here,) * 3,
-        scratch_shapes=[
-            vmem((256, 256), F32), vmem((256, 256), F32), vmem((GROUPS, 4, 32, 256), F32),
-            pltpu.SemaphoreType.DMA((3,)), pltpu.SemaphoreType.DMA((29,)),
-        ],
-    )(output, volume_grad, kg)
+        scratch_shapes=[pltpu.SemaphoreType.DMA((3,))],
+    )(*results)
     return (
         output.reshape(volume.shape),
         volume_grad.reshape(volume.shape),

time: 66.8 us -> 61.3 us (0.918)
  Pallas kernels: 66 us -> 60.4 us
    pallas_call x2, Pallas kernels: 66 us -> 60.4 us  [the longest x1 59.3 us: per_device(): pl.pallas_call(functools.partial(kernel, factor), out_shape=(vmem((256, 2...]
where the time goes in v4:
time: 61.3 us; the launch traced here: 61 us
  Pallas kernels  60.4 us (99%)
  between operations  0.64 us (1%)
    pallas_call x1, Pallas kernels, per_device(): pl.pallas_call(functools.partial(kernel, factor), out_shape=(vmem((256, 2...  59.3 us

profile of v4, /device:TPU:2, one launch (start us, length us, event | category | flops | bytes accessed | tf_op | source)
XLA Modules:
  0.0 61.0 jit_solution(14015936131185753509)
XLA Ops:
  0.6 59.3 %shard_map.58 = (f32[256,256]{1,0:T(8,128)S(1)}, f32[256,256]{1,0:T(8,128)S(1)}, f32[27,32,256]{2,1,0:T(8,128)S(1)}) custom-call(f32[4,8,8,256]{3,2,1,0:T(8,128)} %vol_ref.1, f32[4,8,8,256]{3,2,1,0:T(8,128)} %up_ref.1, f32[27,256,256]{2,1,0:T(8,128)} %bitcast.4), custom_call_target="tpu_custom_call" | custom-call | tf_op jit(solution)/shard_map/pallas_call | solution.py:492
  59.9 1.1 %shard_map.59 = (f32[256,256]{1,0:T(8,128)}, f32[256,256]{1,0:T(8,128)}, f32[27,32,256]{2,1,0:T(8,128)}) custom-call(f32[256,256]{1,0:T(8,128)S(1)} %get-tuple-element.9.out_in, f32[256,256]{1,0:T(8,128)S(1)} %get-tuple-element.10.vg_in, f32[27,32,256]{2,1,0:T(8,128)S(1)} %get-tuple-element.11.kg_in), custom_call_target="tpu_custom_call" | custom-call | tf_op jit(solution)/shard_map/pallas_call | solution.py:505

commit v5 on v4

--- a/solution.py
+++ b/solution.py
@@ -18,6 +18,10 @@
 SLOT = (0, 1, 4, 2, 3, 5, 6)
 BATCHES = ((0, 2), (2, 5), (5, 7))
 N_SEM = 2 * 26 + GROUPS + 6 * (4 + 2 + 3) + (7 + 3 + 3) + len(BATCHES) * (7 + 7 + 3)
+
+
+def far_first(n):
+    return sorted(range(1, n), key=lambda k: -min(k, n - k))
 
 
 def tap(u):
@@ -194,7 +198,7 @@
     def direct(axis, chunk, recv):
         n = 8 if axis == "z" else 4
         return start(*(
-            copy(chunk(step(place(axis), k, n)), recv.at[k - 1], away(axis, k)) for k in range(1, n)
+            copy(chunk(step(place(axis), k, n)), recv.at[k - 1], away(axis, k)) for k in far_first(n)
         ))
 
     def direct_sum(axis, copies, chunk, recv):
@@ -313,7 +317,7 @@
         def e6(self):
             self.c = start(*(
                 copy(low.at[self.sums, step(z, k, 8)], rz.at[k - 1, self.sums], {"dev": step(z, k, 8)})
-                for k in range(1, 8)
+                for k in far_first(8)
             ))
 
         def e7(self):
@@ -329,10 +333,10 @@
             ]
             agz_at(z)[...] = fin[self.all]
             first = counter[0]
-            start(*(copy(fin.at[self.all], agz_at(z), {"dev": step(z, k, 8)}) for k in range(1, 8)))
+            start(*(copy(fin.at[self.all], agz_at(z), {"dev": step(z, k, 8)}) for k in far_first(8)))
             self.c = [
-                self.landed(first + k - 1, agz_at(step(z, -k, 8)), {"dev": step(z, k, 8)})
-                for k in range(1, 8)
+                self.landed(first + i, agz_at(step(z, -k, 8)), {"dev": step(z, k, 8)})
+                for i, k in enumerate(far_first(8))
             ]
 
         def landed(self, i, slot, device):
@@ -347,10 +351,10 @@
             here = agz.at[self.all]
             there = lambda k: rows_of(gathered.at[self.all], k)
             there(y)[...] = agz[self.all]
-            start(*(copy(here, there(y), {"ha": step(y, k, 4)}) for k in range(1, 4)))
+            start(*(copy(here, there(y), {"ha": step(y, k, 4)}) for k in far_first(4)))
             self.c = [
-                self.landed(first + k - 1, there(step(y, -k, 4)), {"ha": step(y, k, 4)})
-                for k in range(1, 4)
+                self.landed(first + i, there(step(y, -k, 4)), {"ha": step(y, k, 4)})
+                for i, k in enumerate(far_first(4))
             ]
 
         def e9(self):
@@ -408,33 +412,35 @@
     groups[6].e2()
     for c in k_copies:
         c.wait()
-    products(0, 8)
+    products(0, 4)
     groups[0].e3()
     groups[1].e3()
-    products(8, 14)
+    products(4, 8)
     groups[3].e3()
     groups[4].e3()
-    products(14, 18)
+    products(8, 10)
     groups[0].e4()
     groups[1].e4()
     batches[0].e6()
-    products(18, 22)
+    products(10, 12)
     groups[5].e3()
     groups[6].e3()
     groups[2].e2()
-    products(22, 24)
+    products(12, 14)
     groups[3].e4()
     groups[4].e4()
     batches[1].e6()
-    products(24, 27)
+    products(14, 18)
     groups[2].e3()
-    batches[0].e7()
     groups[5].e4()
     groups[6].e4()
     batches[2].e6()
+    batches[0].e7()
+    products(18, 22)
     batches[1].e7()
+    batches[2].e7()
     batches[0].e8()
-    batches[2].e7()
+    products(22, 27)
     batches[1].e8()
     batches[2].e8()
     for batch in batches:

time: 61.3 us -> 60.9 us (level)
  no operation moved by 1% of the time
where the time goes in v5:
time: 60.9 us; the launch traced here: 60.5 us
  Pallas kernels  59.9 us (98%)
  between operations  0.64 us (1%)
    pallas_call x1, Pallas kernels, per_device(): pl.pallas_call(functools.partial(kernel, factor), out_shape=(vmem((256, 2...  58.8 us

profile of v5, /device:TPU:2, one launch (start us, length us, event | category | flops | bytes accessed | tf_op | source)
XLA Modules:
  0.0 60.5 jit_solution(10183011547849935572)
XLA Ops:
  0.6 58.8 %shard_map.58 = (f32[256,256]{1,0:T(8,128)S(1)}, f32[256,256]{1,0:T(8,128)S(1)}, f32[27,32,256]{2,1,0:T(8,128)S(1)}) custom-call(f32[4,8,8,256]{3,2,1,0:T(8,128)} %vol_ref.1, f32[4,8,8,256]{3,2,1,0:T(8,128)} %up_ref.1, f32[27,256,256]{2,1,0:T(8,128)} %bitcast.4), custom_call_target="tpu_custom_call" | custom-call | tf_op jit(solution)/shard_map/pallas_call | solution.py:498
  59.4 1.1 %shard_map.59 = (f32[256,256]{1,0:T(8,128)}, f32[256,256]{1,0:T(8,128)}, f32[27,32,256]{2,1,0:T(8,128)}) custom-call(f32[256,256]{1,0:T(8,128)S(1)} %get-tuple-element.9.out_in, f32[256,256]{1,0:T(8,128)S(1)} %get-tuple-element.10.vg_in, f32[27,32,256]{2,1,0:T(8,128)S(1)} %get-tuple-element.11.kg_in), custom_call_target="tpu_custom_call" | custom-call | tf_op jit(solution)/shard_map/pallas_call | solution.py:511

commit v6 on v5

--- a/solution.py
+++ b/solution.py
@@ -17,7 +17,7 @@
 DEPTH = FIRST.index("z")
 SLOT = (0, 1, 4, 2, 3, 5, 6)
 BATCHES = ((0, 2), (2, 5), (5, 7))
-N_SEM = 2 * 26 + GROUPS + 6 * (4 + 2 + 3) + (7 + 3 + 3) + len(BATCHES) * (7 + 7 + 3)
+N_SEM = 2 * 26 + 2 * GROUPS + 6 * (4 + 2 + 3) + (7 + 3 + 3) + len(BATCHES) * (7 + 7 + 3)
 
 
 def far_first(n):
@@ -164,6 +164,8 @@
                     part[g, block % 2, block // 2, 2 * i + half] = res[
                         32 * block : 32 * block + 32, 128 * half : 128 * half + 128
                     ]
+            if i == 1:
+                groups[g].pair()
         for i in range(taps, 4):
             for j in (2 * i, 2 * i + 1):
                 part[g, :, :, j] = jnp.zeros((2, 4, 32, 128), F32)
@@ -242,12 +244,17 @@
             self.g = g
             self.slot = SLOT[g]
             self.sum = summed.at[g]
+            self.pairs = ()
 
         def pair(self):
-            self.c = start(copy(part.at[self.g, 1 - core], pair.at[self.g], {"wa": w + 1 - 2 * core}))
+            h = len(self.pairs)
+            self.pairs += start(copy(
+                part.at[self.g, 1 - core, :, pl.ds(4 * h, 4)], pair.at[self.g, :, pl.ds(4 * h, 4)],
+                {"wa": w + 1 - 2 * core},
+            ))
 
         def add_pair(self):
-            arrive(self.c)
+            arrive(self.pairs)
             self.sum[...] = part[self.g, core] + pair[self.g]
 
     class PlaneGroup(Group):
@@ -390,12 +397,12 @@
     kernel_grad(1)
     arrive(deep_u)
     windows(pad_u, halo_u, wu_hi, wu_lo, range(0, 6, 5))
+    groups[0].e1()
     kernel_grad(2)
-    groups[0].e1()
+    groups[1].e1()
     kernel_grad(3)
-    groups[1].e1()
+    groups[2].e1()
     kernel_grad(4)
-    groups[2].e1()
     groups[3].e1()
     kernel_grad(5)
     groups[4].e1()

time: 60.9 us -> 60.9 us (level)
  no operation moved by 1% of the time
where the time goes in v6:
time: 60.9 us; the launch traced here: 60.5 us
  Pallas kernels  59.8 us (98%)
  between operations  0.64 us (1%)
    pallas_call x1, Pallas kernels, per_device(): pl.pallas_call(functools.partial(kernel, factor), out_shape=(vmem((256, 2...  58.7 us

profile of v6, /device:TPU:2, one launch (start us, length us, event | category | flops | bytes accessed | tf_op | source)
XLA Modules:
  0.0 60.5 jit_solution(4274504723422978775)
XLA Ops:
  0.6 58.7 %shard_map.58 = (f32[256,256]{1,0:T(8,128)S(1)}, f32[256,256]{1,0:T(8,128)S(1)}, f32[27,32,256]{2,1,0:T(8,128)S(1)}) custom-call(f32[4,8,8,256]{3,2,1,0:T(8,128)} %vol_ref.1, f32[4,8,8,256]{3,2,1,0:T(8,128)} %up_ref.1, f32[27,256,256]{2,1,0:T(8,128)} %bitcast.4), custom_call_target="tpu_custom_call" | custom-call | tf_op jit(solution)/shard_map/pallas_call | solution.py:505
  59.4 1.1 %shard_map.59 = (f32[256,256]{1,0:T(8,128)}, f32[256,256]{1,0:T(8,128)}, f32[27,32,256]{2,1,0:T(8,128)}) custom-call(f32[256,256]{1,0:T(8,128)S(1)} %get-tuple-element.9.out_in, f32[256,256]{1,0:T(8,128)S(1)} %get-tuple-element.10.vg_in, f32[27,32,256]{2,1,0:T(8,128)S(1)} %get-tuple-element.11.kg_in), custom_call_target="tpu_custom_call" | custom-call | tf_op jit(solution)/shard_map/pallas_call | solution.py:518

commit v7 on v5

--- a/solution.py
+++ b/solution.py
@@ -404,43 +404,41 @@
     groups[6].e1()
     groups[0].e2()
     groups[1].e2()
-    groups[3].e2()
-    groups[4].e2()
     arrive(halos_v)
     windows(pad_v, halo_v, wv_hi, wv_lo, range(6))
-    groups[5].e2()
-    groups[6].e2()
     for c in k_copies:
         c.wait()
     products(0, 4)
+    groups[3].e2()
+    groups[4].e2()
+    products(4, 10)
+    groups[5].e2()
+    groups[6].e2()
+    products(10, 12)
     groups[0].e3()
     groups[1].e3()
-    products(4, 8)
+    products(12, 14)
     groups[3].e3()
     groups[4].e3()
-    products(8, 10)
+    groups[2].e2()
+    groups[5].e3()
+    groups[6].e3()
+    products(14, 18)
     groups[0].e4()
     groups[1].e4()
     batches[0].e6()
-    products(10, 12)
-    groups[5].e3()
-    groups[6].e3()
-    groups[2].e2()
-    products(12, 14)
     groups[3].e4()
     groups[4].e4()
     batches[1].e6()
-    products(14, 18)
     groups[2].e3()
     groups[5].e4()
     groups[6].e4()
     batches[2].e6()
+    products(18, 27)
     batches[0].e7()
-    products(18, 22)
     batches[1].e7()
     batches[2].e7()
     batches[0].e8()
-    products(22, 27)
     batches[1].e8()
     batches[2].e8()
     for batch in batches:

time: 60.9 us -> 60.6 us (level)
  Pallas kernels: 59.9 us -> 59.2 us
    pallas_call x1, Pallas kernels: 58.8 us -> 58.1 us  [per_device(): pl.pallas_call(functools.partial(kernel, factor), out_shape=(vmem((256, 2...]
where the time goes in v7:
time: 60.6 us; the launch traced here: 59.8 us
  Pallas kernels  59.2 us (98%)
  between operations  0.64 us (1%)
    pallas_call x1, Pallas kernels, per_device(): pl.pallas_call(functools.partial(kernel, factor), out_shape=(vmem((256, 2...  58.1 us

profile of v7, /device:TPU:2, one launch (start us, length us, event | category | flops | bytes accessed | tf_op | source)
XLA Modules:
  0.0 59.8 jit_solution(1834916932195678102)
XLA Ops:
  0.6 58.1 %shard_map.58 = (f32[256,256]{1,0:T(8,128)S(1)}, f32[256,256]{1,0:T(8,128)S(1)}, f32[27,32,256]{2,1,0:T(8,128)S(1)}) custom-call(f32[4,8,8,256]{3,2,1,0:T(8,128)} %vol_ref.1, f32[4,8,8,256]{3,2,1,0:T(8,128)} %up_ref.1, f32[27,256,256]{2,1,0:T(8,128)} %bitcast.4), custom_call_target="tpu_custom_call" | custom-call | tf_op jit(solution)/shard_map/pallas_call | solution.py:496
  58.7 1.1 %shard_map.59 = (f32[256,256]{1,0:T(8,128)}, f32[256,256]{1,0:T(8,128)}, f32[27,32,256]{2,1,0:T(8,128)}) custom-call(f32[256,256]{1,0:T(8,128)S(1)} %get-tuple-element.9.out_in, f32[256,256]{1,0:T(8,128)S(1)} %get-tuple-element.10.vg_in, f32[27,32,256]{2,1,0:T(8,128)S(1)} %get-tuple-element.11.kg_in), custom_call_target="tpu_custom_call" | custom-call | tf_op jit(solution)/shard_map/pallas_call | solution.py:509
